TPU v7x, 128 devices: a whole 4x4x4 slice. The times are simulated.
128 devices in a mesh: row: 8 (over z, y_lo), col: 16 (over x, y_hi, core).
Axes of the slice: x: 4, y: 4 (y_hi: 2, y_lo: 2; y = y_hi * 2 + y_lo), z: 4, core: 2. Of those that a mesh axis runs over, the one named last changes fastest.
Arguments:
- integrals: bfloat16 [10240, 10240], P('row', 'col'), may hold values from -6 to 6
- amplitudes: bfloat16 [10240, 8192], P('row', 'col'), may hold values from -0.0625 to 0.0625
- int_shape: int32 [40, 40], P('row'), may hold values 0 or 1
- amp_shape: int32 [40, 32], P(None, 'col'), may hold values 0 or 1
Outputs:
- ladder: bfloat16 [10240, 8192], P('row', 'col')
All inputs are finite; a program needn't handle non-finite values. No bound on the sum of `int_shape` or of `amp_shape` on one device may be relied on, other than what follows from the above.
Results may differ from a plain program's by a relative error of at most 0.001.
Values may be sent and summed in bfloat16 or wider, within the bound.
No kernel may reach another device: no remote copies, remote signals or barrier semaphores. Data moves between devices by JAX's collectives and lax.ppermute only.
A program may use at most 192 MiB of HBM per device.

v0:
```python
import jax
import jax.numpy as jnp
from jax import lax
from jax.sharding import PartitionSpec as P

TILE = 256


def expand_shape(shape_mask):
    return jnp.repeat(jnp.repeat(shape_mask, TILE, axis=0), TILE, axis=1).astype(jnp.bfloat16)


def per_device(integrals, amplitudes, int_shape, amp_shape):
    int_mask = expand_shape(int_shape)
    amp_mask = expand_shape(amp_shape)
    whole_amp = lax.all_gather(amplitudes, "row", axis=0, tiled=True) * amp_mask
    left = lax.all_gather(integrals, "col", axis=1, tiled=True) * int_mask
    total = jnp.dot(left, whole_amp, preferred_element_type=jnp.float32)
    return total.astype(jnp.bfloat16)


def solution(mesh):
    in_specs = (P("row", "col"), P("row", "col"), P("row", None), P(None, "col"))
    out_specs = P("row", "col")
    return jax.shard_map(
        per_device, mesh=mesh, in_specs=in_specs, out_specs=out_specs, check_vma=False
    )
```

profile of v0, /device:TPU:1, one launch (start us, length us, event | category | flops | bytes accessed | tf_op | source)
XLA Modules:
  0.0 410.5 jit_solution(6335129066689984502)
XLA Ops:
  6.5 0.0 all-gather.5.cloned.1.call-start
  6.5 0.7 all-gather.5.cloned.1.call-update
  7.3 0.0 all-gather.3.cloned.1.call-start
  7.3 0.7 all-gather.3.cloned.1.call-update
  8.0 0.7 convert_element_type.25
  8.7 12.1 %broadcast_in_dim.13 = bf16[1280,40,256]{2,1,0:T(8,128)(2,1)} broadcast(bf16[1280,40]{1,0:T(8,128)(2,1)S(1)} %bitcast.11), dimensions={0,1} | broadcast | bytes 26316800 | tf_op jit(solution)/shard_map/broadcast_in_dim | solution.py:10
  20.8 0.0 copy-start
  20.8 23.5 %copy.6 = bf16[160,8,40,256]{3,1,2,0:T(8,128)(2,1)} copy(bf16[160,8,40,256]{3,2,1,0:T(8,128)(2,1)} %bitcast.6) | data formatting | bytes 52428800
  44.3 0.0 copy-done
  44.3 0.1 copy.5
  44.4 0.3 broadcast_in_dim.14
  44.8 12.5 %broadcast_in_dim.15 = bf16[10240,2,256]{2,1,0:T(2,128)(2,1)S(1)} broadcast(bf16[10240,2]{1,0:T(8,128)(2,1)S(1)} %bitcast.10), dimensions={0,1} | broadcast | bytes 10526720 | tf_op jit(solution)/shard_map/broadcast_in_dim | solution.py:10
  57.3 7.3 %copy.7 = bf16[1280,8,2,256]{3,1,2,0:T(8,128)(2,1)} copy(bf16[1280,8,2,256]{3,2,1,0:T(2,128)(2,1)S(1)} %bitcast.7) | data formatting | bytes 20971520
  64.6 155.3 %all-gather.5.cloned.1.call-done = bf16[10240,512]{1,0:T(8,128)(2,1)} async-done(((bf16[1280,512]{1,0:T(8,128)(2,1)}), bf16[10240,512]{1,0:T(8,128)(2,1)}) %all-gather.5.cloned.1.call-update) | async-done | bytes 10485776 | tf_op jit(solution)/shard_map/all_gather | solution.py:16
  219.9 156.8 %all-gather.3.cloned.1.call-done = bf16[1280,10240]{1,0:T(8,128)(2,1)} async-done(((bf16[1280,640]{1,0:T(8,128)(2,1)}), bf16[1280,10240]{1,0:T(8,128)(2,1)}) %all-gather.3.cloned.1.call-update) | async-done | bytes 26214416 | tf_op jit(solution)/shard_map/all_gather | solution.py:17
  376.7 27.0 %fusion.3 = bf16[1280,512]{1,0:T(8,128)(2,1)} fusion(bf16[10240,512]{1,0:T(8,128)(2,1)} %all-gather.5.cloned.1.call-done, bf16[10240,512]{1,0:T(8,128)(2,1)} %bitcast.9, bf16[1280,10240]{1,0:T(8,128)(2,1)} %all-gather.3.cloned.1.call-done, bf16[1280,10240]{1,0:T(8,128)(2,1)} %bitcast.8), kind=kOutput, calls=%fused_computation.3 | convolution fusion | flops 13440778240 | bytes 74711040 | tf_op jit(solution)/shard_map/dot_general | solution.py:18
  (2 shorter events, 0.1 us)
Async XLA Ops:
  6.5 213.4 %all-gather.5.cloned.1.call-start = ((), (), s32[]{:S(2)}) async-start(), calls=%async_computation.1 | async-start | bytes 11796480 | tf_op jit(solution)/shard_map/all_gather | solution.py:16
  7.3 369.4 %all-gather.3.cloned.1.call-start = ((), (), s32[]{:S(2)}) async-start(), calls=%async_computation | async-start | bytes 27852800 | tf_op jit(solution)/shard_map/all_gather | solution.py:17
  20.8 23.5 %copy-start = (s32[40,2]{0,1:T(2,128)S(1)}, s32[40,2]{0,1:T(2,128)}, u32[]{:S(2)}) copy-start(s32[40,2]{0,1:T(2,128)} %param.7) | copy-start | bytes 964
Sparse Core Ops, SparseCore 0:
  9.0 210.8 all-gather.4
  222.4 154.2 all-gather.2
where the time goes:
time: 411 us
  waiting for transfers between devices  314 us (76%)
  local copies, waits for them, and re-layouts  55.8 us (14%)
  matrix products  27 us (7%)
  between operations  13.4 us (3%)
    all_gather x1, waiting for transfers between devices, per_device(): left = lax.all_gather(integrals, 'col', axis=1, tiled=True) * int_mask  157 us
    all_gather x1, waiting for transfers between devices, per_device(): whole_amp = lax.all_gather(amplitudes, 'row', axis=0, tiled=True) * amp_mask  155 us
    unnamed x4, local copies, waits for them, and re-layouts  30.7 us
    dot_general x1, matrix products, per_device(): total = jnp.dot(left, whole_amp, preferred_element_type=jnp.float32)  27 us
    broadcast_in_dim x2, local copies, waits for them, and re-layouts, expand_shape(): jnp.repeat(jnp.repeat(shape_mask, TILE, axis=0), TILE, axis=1)  24.6 us
  transfers between devices with their start and end apart: 2, of which 2 were waited for; matrix products, arithmetic and copies ran while one was open for 14% of the time, Pallas kernels for 0%

commit v1 on v0

v1 whole, which is shorter than its diff:
```python
import functools

import jax
import jax.numpy as jnp
from jax import lax
from jax.experimental import pallas as pl
from jax.experimental.pallas import tpu as pltpu
from jax.sharding import Mesh, PartitionSpec as P

TILE = 256
AXES = ("z", "ylo", "x", "yhi", "core")
NX, NY, NZ = 4, 4, 4


def flat(z, y, x, c):
    z, y, x = z % NZ, y % NY, x % NX
    return (((z * 2 + y % 2) * NX + x) * 2 + y // 2) * 2 + c


def pairs_of(move):
    return [
        (flat(z, y, x, c), flat(*move(z, y, x, c)))
        for z in range(NZ)
        for y in range(NY)
        for x in range(NX)
        for c in range(2)
    ]


def sign(c):
    return 1 - 2 * c


X_AHEAD = pairs_of(lambda z, y, x, c: (z, y, x + sign(c), c))
X_BACK = pairs_of(lambda z, y, x, c: (z, y, x - sign(c), c))
Z_AHEAD = pairs_of(lambda z, y, x, c: (z + sign(c), y, x, c))
Z_BACK = pairs_of(lambda z, y, x, c: (z - sign(c), y, x, c))
Y_FAR = pairs_of(lambda z, y, x, c: (z, y + 2, x, c))
Y_NEAR = pairs_of(lambda z, y, x, c: (z, y ^ 1, x, c))
SWAP = pairs_of(lambda z, y, x, c: (z, y, x, 1 - c))


def send(value, pairs):
    return lax.ppermute(value, AXES, pairs)


def after(value, *earlier):
    return lax.optimization_barrier((value, *earlier))[0]


def mask_kernel(meta, amp_shape, b_ref, mine, other):
    chunk = TILE // 2
    count = mine.shape[0] // chunk
    for out, half in ((mine, meta[0]), (other, 1 - meta[0])):
        for i in range(count):
            source = half * count + i
            rows = pl.ds(pl.multiple_of(source * chunk, chunk), chunk)
            tile_row = meta[1] + source // 2
            for q in range(amp_shape.shape[1]):
                cols = pl.ds(q * TILE, TILE)
                value = b_ref[rows, cols]
                keep = amp_shape[tile_row, q] != 0
                out[pl.ds(i * chunk, chunk), cols] = jnp.where(keep, value, jnp.zeros_like(value))


def mask_halves(core, first, amp_shape, b):
    half = jax.ShapeDtypeStruct((b.shape[0] // 2, b.shape[1]), b.dtype)
    return pl.pallas_call(
        mask_kernel,
        out_shape=(half, half),
        in_specs=[pl.BlockSpec(memory_space=pltpu.SMEM)] * 2
        + [pl.BlockSpec(memory_space=pltpu.VMEM)],
        out_specs=[pl.BlockSpec(memory_space=pltpu.VMEM)] * 2,
        cost_estimate=pl.CostEstimate(flops=0, bytes_accessed=4 * b.size, transcendentals=0),
    )(jnp.stack([core, first]).astype(jnp.int32), amp_shape, b)


def block_kernel(n_groups, n_b, sides, has_acc, *refs):
    meta, int_shape = refs[:2]
    a_refs = refs[2 : 2 + n_groups]
    b_refs = refs[2 + n_groups : 2 + n_groups + n_b]
    rest = refs[2 + n_groups + n_b :]
    if has_acc:
        acc_in, rest = rest[0], rest[1:]
    out, a_buf, b_buf, acc, a_sem, b_sem, c_sem = rest
    slots, depth = a_buf.shape[0], a_buf.shape[2] // 2
    chunk = TILE // 2

    def a_copy(g):
        slot, part = g // 2 % slots, g % 2
        return pltpu.make_async_copy(
            a_refs[g], a_buf.at[slot, :, pl.ds(part * depth, depth)], a_sem.at[slot, part]
        )

    def b_copy(j, g):
        slot, part = g // 2 % slots, g % 2
        source = b_refs[j]
        if len(sides) == 1:
            source = source.at[pl.ds(sides[0], 1)]
        return pltpu.make_async_copy(
            source, b_buf.at[slot, :, pl.ds(part * depth, depth)], b_sem.at[slot, part]
        )

    def start(pair):
        for g in (2 * pair, 2 * pair + 1):
            for j in range(n_b):
                @pl.when(meta[1 + n_groups + j] == meta[1 + g])
                def _():
                    b_copy(j, g).start()
            a_copy(g).start()

    pairs = n_groups // 2
    for pair in range(min(slots, pairs)):
        start(pair)
    if has_acc:
        source = acc_in.at[pl.ds(sides[0], 1)] if len(sides) == 1 else acc_in
        acc_copy = pltpu.make_async_copy(source, acc, c_sem)
        acc_copy.start()
        acc_copy.wait()

    for pair in range(pairs):
        slot = pair % slots
        for g in (2 * pair, 2 * pair + 1):
            b_copy(0, g).wait()
            a_copy(g).wait()
        first = [(2 * meta[1 + g] + meta[0]) * (depth // chunk) for g in (2 * pair, 2 * pair + 1)]
        for p in range(int_shape.shape[0]):
            rows = pl.ds(p * TILE, TILE)
            parts = []
            for h in range(2):
                for j in range(depth // chunk):
                    value = a_buf[slot, rows, pl.ds(h * depth + j * chunk, chunk)]
                    keep = int_shape[p, (first[h] + j) // 2] != 0
                    parts.append(jnp.where(keep, value, jnp.zeros_like(value)))
            left = jnp.concatenate(parts, axis=1)
            for i in range(len(sides)):
                total = jnp.dot(left, b_buf[slot, i], preferred_element_type=jnp.float32)
                if pair > 0 or has_acc:
                    total = total + acc[i, rows, :]
                acc[i, rows, :] = total
        if pair + slots < pairs:
            start(pair + slots)
    out_copy = pltpu.make_async_copy(acc, out, c_sem)
    out_copy.start()
    out_copy.wait()


def block_matmul(core, int_shape, groups, b_blocks, sides, acc=None):
    a_refs, a_of = [g[0] for g in groups], [g[1] for g in groups]
    b_refs, b_of = [b[0] for b in b_blocks], [b[1] for b in b_blocks]
    rows, depth = a_refs[0].shape
    columns = b_refs[0].shape[2]
    n = len(groups)
    slots = min(2, n // 2)
    meta = jnp.stack([core] + a_of + b_of).astype(jnp.int32)
    operands = [meta, int_shape] + a_refs + b_refs + ([] if acc is None else [acc])
    in_specs = [pl.BlockSpec(memory_space=pltpu.SMEM)] * 2
    in_specs += [pl.BlockSpec(memory_space=pltpu.HBM)] * (len(operands) - 2)
    return pl.pallas_call(
        functools.partial(block_kernel, n, len(b_refs), sides, acc is not None),
        out_shape=jax.ShapeDtypeStruct((len(sides), rows, columns), jnp.float32),
        in_specs=in_specs,
        out_specs=pl.BlockSpec(memory_space=pltpu.HBM),
        scratch_shapes=[
            pltpu.VMEM((slots, rows, 2 * depth), jnp.bfloat16),
            pltpu.VMEM((slots, len(sides), 2 * depth, columns), jnp.bfloat16),
            pltpu.VMEM((len(sides), rows, columns), jnp.float32),
            pltpu.SemaphoreType.DMA((slots, 2)),
            pltpu.SemaphoreType.DMA((slots, 2)),
            pltpu.SemaphoreType.DMA,
        ],
        cost_estimate=pl.CostEstimate(
            flops=2 * rows * depth * columns * n * len(sides),
            bytes_accessed=n * 2 * depth * (rows + len(sides) * columns),
            transcendentals=0,
        ),
    )(*operands)


def per_device(a, b, int_shape, amp_shape):
    z, ylo, x = lax.axis_index("z"), lax.axis_index("ylo"), lax.axis_index("x")
    yhi, core = lax.axis_index("yhi"), lax.axis_index("core")
    step = sign(core)
    barrier = lax.optimization_barrier

    x1 = send(a, X_AHEAD)
    x2 = send(a, X_BACK)
    aq = send(a, Y_FAR)
    mine, other = mask_halves(core, (2 * z + ylo) * (b.shape[0] // TILE), amp_shape, b)
    b0 = jnp.stack([mine, send(other, SWAP)])
    z1 = send(b0, Z_AHEAD)
    z2 = send(b0, Z_BACK)
    a0, b0, x1, x2, aq, z1, z2 = barrier((a, b0, x1, x2, aq, z1, z2))

    x3 = send(x1, X_AHEAD)
    x4 = send(aq, X_AHEAD)
    z3 = send(z1, Z_AHEAD)
    bq = send(b0, Y_NEAR)
    b0, aq, x3, x4, z3, bq = barrier((b0, aq, x3, x4, z3, bq))

    x5 = send(aq, X_BACK)
    x6 = send(x4, X_AHEAD)
    z4 = send(bq, Z_AHEAD)
    z5 = send(bq, Z_BACK)
    z6 = send(z3, Y_NEAR)

    spots = [x, (x - step) % NX, (x + step) % NX, (x + 2) % NX]
    group_of = [2 * s + yhi for s in spots] + [2 * s + 1 - yhi for s in spots]
    groups = list(zip([a0, x1, x2, x3, aq, x4, x5, x6], group_of))
    deep = [z, (z - step) % NZ, (z + step) % NZ, (z + 2) % NZ]
    b_of = [2 * s + ylo for s in deep] + [2 * s + 1 - ylo for s in deep]
    b_blocks = list(zip([b0, z1, z2, z3, bq, z4, z5, z6], b_of))

    early = block_matmul(core, int_shape, groups[:6], b_blocks, (0, 1))
    theirs = block_matmul(core, int_shape, groups[6:], b_blocks, (1,), early)
    got = send(theirs, SWAP)
    ours = block_matmul(core, int_shape, groups[6:], b_blocks, (0,), early)
    return (ours + got)[0].astype(jnp.bfloat16)


def solution(mesh):
    fine = Mesh(mesh.devices.reshape(NZ, 2, NX, 2, 2), AXES)
    row, col = ("z", "ylo"), ("x", "yhi", "core")
    return jax.shard_map(
        per_device,
        mesh=fine,
        in_specs=(P(row, col), P(row, col), P(row, None), P(None, col)),
        out_specs=P(row, col),
        check_vma=False,
    )
```

time: 411 us -> 158 us (0.38)
  waiting for transfers between devices: 314 us -> 85.8 us
  local copies, waits for them, and re-layouts: 55.8 us -> 3.8 us
  Pallas kernels: 0 us -> 34.1 us
  starting transfers between devices: 0.04 us -> 28.3 us
  matrix products: 27 us -> 0 us
  between operations: 13.4 us -> 0.13 us
  other arithmetic: 0.7 us -> 5.06 us
    all_gather x2 -> x0, waiting for transfers between devices: 312 us -> none  [the longest x1 157 us: per_device(): left = lax.all_gather(integrals, 'col', axis=1, tiled=True) * int_mask]
    ppermute x0 -> x16, waiting for transfers between devices: none -> 85.8 us  [send(): return lax.ppermute(value, AXES, pairs)]
    pallas_call x0 -> x4, Pallas kernels: none -> 34.1 us  [the longest x3 31.6 us: block_matmul(): pl.pallas_call(functools.partial(block_kernel, n, len(b_refs), sides, acc...]
    ppermute x0 -> x16, starting transfers between devices: none -> 28.3 us  [send(): return lax.ppermute(value, AXES, pairs)]
    unnamed x4 -> x15, local copies, waits for them, and re-layouts: 30.7 us -> 2.52 us
    dot_general x1 -> x0, matrix products: 27 us -> none  [per_device(): total = jnp.dot(left, whole_amp, preferred_element_type=jnp.float32)]
    broadcast_in_dim x4 -> x0, local copies, waits for them, and re-layouts: 25 us -> none  [the longest x2 24.6 us: expand_shape(): jnp.repeat(jnp.repeat(shape_mask, TILE, axis=0), TILE, axis=1)]
  transfers between devices with their start and end apart: 2 -> 16, of which waited for: 2 -> 8; matrix products, arithmetic and copies ran while one was open for 14% -> 2% of each run, Pallas kernels for 0% -> 16%
where the time goes in v1:
time: 158 us; the launch traced here: 157 us
  waiting for transfers between devices  85.8 us (54%)
  Pallas kernels  34.1 us (22%)
  starting transfers between devices  28.3 us (18%)
  other arithmetic  5.06 us (3%)
  local copies, waits for them, and re-layouts  3.8 us (2%)
    ppermute x16, waiting for transfers between devices, send(): return lax.ppermute(value, AXES, pairs)  85.8 us
    pallas_call x3, Pallas kernels, block_matmul(): pl.pallas_call(functools.partial(block_kernel, n, len(b_refs), sides, acc...  31.6 us
    ppermute x16, starting transfers between devices, send(): return lax.ppermute(value, AXES, pairs)  28.3 us
    convert_element_type x1, other arithmetic, per_device(): return (ours + got)[0].astype(jnp.bfloat16)  3.24 us
  transfers between devices with their start and end apart: 16, of which 8 were waited for; matrix products, arithmetic and copies ran while one was open for 2% of the time, Pallas kernels for 16%

profile of v1, /device:TPU:1, one launch (start us, length us, event | category | flops | bytes accessed | tf_op | source)
XLA Modules:
  0.0 157.2 jit_solution(12188492666060865921)
XLA Ops:
  0.0 1.4 copy.5.amp_shape
  1.4 0.6 pad_add_fusion.meta
  2.0 2.5 %shard_map.46 = (bf16[640,512]{1,0:T(8,128)(2,1)}, bf16[640,512]{1,0:T(8,128)(2,1)}) custom-call(s32[2]{0:T(128)} %pad_add_fusion.meta, s32[40,2]{1,0:T(8,128)} %copy.5.amp_shape, bf16[1280,512]{1,0:T(8,128)(2,1)} %b_ref.1), custom_call_target="tpu_custom_call" | custom-call | bytes 2621440 | tf_op jit(solution)/shard_map/pallas_call | solution.py:68
  4.5 1.4 collective-permute-start
  5.9 1.3 collective-permute-start.2
  7.2 1.4 collective-permute-start.1
  8.6 3.0 %collective-permute-start.3 = (bf16[1280,640]{1,0:T(8,128)(2,1)}, bf16[1280,640]{1,0:T(8,128)(2,1)}, u32[]{:S(2)}, u32[]{:S(2)}) collective-permute-start(bf16[1280,640]{1,0:T(8,128)(2,1)} %refs_2_), channel_id=1, source_target_pairs={{0,2},{1,3},{4,6},{5,7},{8,10},{9,11},{12,14},{13,15},{16,18},{17,... | collective-permute-start | bytes 4915208 | tf_op jit(solution)/shard_map/ppermute | solution.py:44
  11.6 1.2 pad_maximum_fusion.refs_8_.refs_4_
  12.8 1.7 %collective-permute-start.5 = (bf16[2,640,512]{2,1,0:T(8,128)(2,1)S(1)}, bf16[2,640,512]{2,1,0:T(8,128)(2,1)S(1)}, u32[]{:S(2)}, u32[]{:S(2)}) collective-permute-start(bf16[2,640,512]{2,1,0:T(8,128)(2,1)S(1)} %pad_maximum_fusion.refs_8_.refs_4_), channel_id=1, source_target_pairs={{0,96},{1,33},{4,100},{5,37},{8,104},{9,41},{12,108},{13,45},{16,1... | collective-permute-start | bytes 3932168 | tf_op jit(solution)/shard_map/ppermute | solution.py:44
  14.5 2.2 %collective-permute-start.4 = (bf16[2,640,512]{2,1,0:T(8,128)(2,1)S(1)}, bf16[2,640,512]{2,1,0:T(8,128)(2,1)S(1)}, u32[]{:S(2)}, u32[]{:S(2)}) collective-permute-start(bf16[2,640,512]{2,1,0:T(8,128)(2,1)S(1)} %pad_maximum_fusion.refs_8_.refs_4_), channel_id=1, source_target_pairs={{0,32},{1,97},{4,36},{5,101},{8,40},{9,105},{12,44},{13,109},{16,4... | collective-permute-start | bytes 3932168 | tf_op jit(solution)/shard_map/ppermute | solution.py:44
  16.7 25.1 %collective-permute-done.2.refs_4_ = bf16[1280,640]{1,0:T(8,128)(2,1)S(1)} collective-permute-done((bf16[1280,640]{1,0:T(8,128)(2,1)}, bf16[1280,640]{1,0:T(8,128)(2,1)S(1)}, u32[]{:S(2)}, u32[]{:S(2)}) %collective-permute-start.2) | collective-permute-done | bytes 1638432 | tf_op jit(solution)/shard_map/ppermute | solution.py:44
  41.9 2.6 %collective-permute-done.1.refs_3_ = bf16[1280,640]{1,0:T(8,128)(2,1)S(1)} collective-permute-done((bf16[1280,640]{1,0:T(8,128)(2,1)}, bf16[1280,640]{1,0:T(8,128)(2,1)S(1)}, u32[]{:S(2)}, u32[]{:S(2)}) %collective-permute-start.1) | collective-permute-done | bytes 1638432 | tf_op jit(solution)/shard_map/ppermute | solution.py:44
  44.5 3.3 %collective-permute-done.3.refs_6_ = bf16[1280,640]{1,0:T(8,128)(2,1)} collective-permute-done((bf16[1280,640]{1,0:T(8,128)(2,1)}, bf16[1280,640]{1,0:T(8,128)(2,1)}, u32[]{:S(2)}, u32[]{:S(2)}) %collective-permute-start.3) | collective-permute-done | bytes 1638432 | tf_op jit(solution)/shard_map/ppermute | solution.py:44
  47.9 1.3 collective-permute-start.6
  49.2 1.3 collective-permute-start.9
  50.5 3.8 %collective-permute-start.8 = (bf16[2,640,512]{2,1,0:T(8,128)(2,1)S(1)}, bf16[2,640,512]{2,1,0:T(8,128)(2,1)}, u32[]{:S(2)}, u32[]{:S(2)}) collective-permute-start(bf16[2,640,512]{2,1,0:T(8,128)(2,1)S(1)} %collective-permute-done.4.refs_9_.refs_5_), channel_id=1, source_target_pairs={{0,32},{1,97},{4,36},{5,101},{8,40},{9,105},{12,44},{13,109},{16,4... | collective-permute-start | bytes 3932168 | tf_op jit(solution)/shard_map/ppermute | solution.py:44
  54.2 24.0 %collective-permute-done.9.refs_12_.refs_8_ = bf16[2,640,512]{2,1,0:T(8,128)(2,1)} collective-permute-done((bf16[2,640,512]{2,1,0:T(8,128)(2,1)S(1)}, bf16[2,640,512]{2,1,0:T(8,128)(2,1)}, u32[]{:S(2)}, u32[]{:S(2)}) %collective-permute-start.9) | collective-permute-done | bytes 1310752 | tf_op jit(solution)/shard_map/ppermute | solution.py:44
  78.2 7.7 %collective-permute-done.6.refs_5_ = bf16[1280,640]{1,0:T(8,128)(2,1)S(1)} collective-permute-done((bf16[1280,640]{1,0:T(8,128)(2,1)S(1)}, bf16[1280,640]{1,0:T(8,128)(2,1)S(1)}, u32[]{:S(2)}, u32[]{:S(2)}) %collective-permute-start.6) | collective-permute-done | bytes 1638432 | tf_op jit(solution)/shard_map/ppermute | solution.py:44
  85.9 1.4 collective-permute-start.14
  87.3 1.6 %collective-permute-start.13 = (bf16[2,640,512]{2,1,0:T(8,128)(2,1)}, bf16[2,640,512]{2,1,0:T(8,128)(2,1)}, u32[]{:S(2)}, u32[]{:S(2)}) collective-permute-start(bf16[2,640,512]{2,1,0:T(8,128)(2,1)} %collective-permute-done.9.refs_12_.refs_8_), channel_id=1, source_target_pairs={{0,96},{1,33},{4,100},{5,37},{8,104},{9,41},{12,108},{13,45},{16,1... | collective-permute-start | bytes 3932168 | tf_op jit(solution)/shard_map/ppermute | solution.py:44
  88.9 2.1 %collective-permute-start.12 = (bf16[2,640,512]{2,1,0:T(8,128)(2,1)}, bf16[2,640,512]{2,1,0:T(8,128)(2,1)}, u32[]{:S(2)}, u32[]{:S(2)}) collective-permute-start(bf16[2,640,512]{2,1,0:T(8,128)(2,1)} %collective-permute-done.9.refs_12_.refs_8_), channel_id=1, source_target_pairs={{0,32},{1,97},{4,36},{5,101},{8,40},{9,105},{12,44},{13,109},{16,4... | collective-permute-start | bytes 3932168 | tf_op jit(solution)/shard_map/ppermute | solution.py:44
  91.1 2.9 %collective-permute-start.11 = (bf16[1280,640]{1,0:T(8,128)(2,1)}, bf16[1280,640]{1,0:T(8,128)(2,1)}, u32[]{:S(2)}, u32[]{:S(2)}) collective-permute-start(bf16[1280,640]{1,0:T(8,128)(2,1)} %collective-permute-done.7.refs_7_), channel_id=1, source_target_pairs={{0,4},{1,13},{4,8},{5,1},{8,12},{9,5},{12,0},{13,9},{16,20},{17,29... | collective-permute-start | bytes 4915208 | tf_op jit(solution)/shard_map/ppermute | solution.py:44
  94.0 0.7 stack.105.refs_0_
  94.6 0.6 stack.117.refs_0_
  95.2 18.3 %collective-permute-done.14.refs_15_.refs_11_ = bf16[2,640,512]{2,1,0:T(8,128)(2,1)} collective-permute-done((bf16[2,640,512]{2,1,0:T(8,128)(2,1)}, bf16[2,640,512]{2,1,0:T(8,128)(2,1)}, u32[]{:S(2)}, u32[]{:S(2)}) %collective-permute-start.14) | collective-permute-done | bytes 1310752 | tf_op jit(solution)/shard_map/ppermute | solution.py:44
  114.0 4.4 %collective-permute-done.12.refs_13_.refs_9_ = bf16[2,640,512]{2,1,0:T(8,128)(2,1)} collective-permute-done((bf16[2,640,512]{2,1,0:T(8,128)(2,1)}, bf16[2,640,512]{2,1,0:T(8,128)(2,1)}, u32[]{:S(2)}, u32[]{:S(2)}) %collective-permute-start.12) | collective-permute-done | bytes 1310752 | tf_op jit(solution)/shard_map/ppermute | solution.py:44
  118.3 17.1 %shard_map.47.refs_12_ = f32[2,1280,512]{2,1,0:T(8,128)} custom-call(s32[15]{0:T(128)} %stack.117.refs_0_, s32[5,40]{1,0:T(8,128)} %refs_1_.5, bf16[1280,640]{1,0:T(8,128)(2,1)} %refs_2_, bf16[1280,640]{1,0:T(8,128)(2,1)} %copy-done.5, bf16[1280,640]{1,0:T(8,128)(2,1)} %copy-done.4, bf16[1280,640]{1,0:T(8,128)(2,1)} %copy-done.6, ...), custom_call_target="tpu_custom_call" | custom-call | flops 10066329600 | bytes 17694720 | tf_op jit(solution)/shard_map/pallas_call | solution.py:159
  135.5 1.1 copy-done.1
  136.6 7.2 %shard_map.49 = f32[1,1280,512]{2,1,0:T(8,128)} custom-call(s32[11]{0:T(128)} %stack.105.refs_0_, s32[5,40]{1,0:T(8,128)} %refs_1_.5, bf16[1280,640]{1,0:T(8,128)(2,1)} %copy-done.1, bf16[1280,640]{1,0:T(8,128)(2,1)} %collective-permute-done.11.refs_3_, bf16[2,640,512]{2,1,0:T(8,128)(2,1)} %copy-done, bf16[2,640,512]{2,1,0:T(8,128)(2,1)} %copy-done.3, ...), custom_call_target="tpu_custom_call" | custom-call | flops 1677721600 | bytes 4587520 | tf_op jit(solution)/shard_map/pallas_call | solution.py:159
  143.9 2.8 %collective-permute-start.15 = (f32[1,1280,512]{2,1,0:T(8,128)}, f32[1,1280,512]{2,1,0:T(8,128)S(1)}, u32[]{:S(2)}, u32[]{:S(2)}) collective-permute-start(f32[1,1280,512]{2,1,0:T(8,128)} %shard_map.49), channel_id=1, source_target_pairs={{0,1},{1,0},{4,5},{5,4},{8,9},{9,8},{12,13},{13,12},{16,17},{17,16... | collective-permute-start | bytes 7864328 | tf_op jit(solution)/shard_map/ppermute | solution.py:44
  146.7 7.3 %shard_map.48 = f32[1,1280,512]{2,1,0:T(8,128)} custom-call(s32[11]{0:T(128)} %stack.105.refs_0_, s32[5,40]{1,0:T(8,128)} %refs_1_.5, bf16[1280,640]{1,0:T(8,128)(2,1)} %copy-done.1, bf16[1280,640]{1,0:T(8,128)(2,1)} %collective-permute-done.11.refs_3_, bf16[2,640,512]{2,1,0:T(8,128)(2,1)} %copy-done, bf16[2,640,512]{2,1,0:T(8,128)(2,1)} %copy-done.3, ...), custom_call_target="tpu_custom_call" | custom-call | flops 1677721600 | bytes 4587520 | tf_op jit(solution)/shard_map/pallas_call | solution.py:159
  154.0 3.2 %fusion = bf16[1280,512]{1,0:T(8,128)(2,1)} fusion(f32[1,1280,512]{2,1,0:T(8,128)} %shard_map.48, f32[1,1280,512]{2,1,0:T(8,128)S(1)} %collective-permute-done.15), kind=kLoop, calls=%fused_computation.1 | loop fusion | flops 1310720 | bytes 6553600 | tf_op jit(solution)/shard_map/convert_element_type | solution.py:218
  (24 shorter events, 0.6 us)
Async XLA Ops:
  4.5 7.1 %collective-permute-start = (bf16[640,512]{1,0:T(8,128)(2,1)}, bf16[640,512]{1,0:T(8,128)(2,1)S(1)}, u32[]{:S(2)}, u32[]{:S(2)}) collective-permute-start(bf16[640,512]{1,0:T(8,128)(2,1)} %get-tuple-element.21), channel_id=1, source_target_pairs={{0,1},{1,0},{4,5},{5,4},{8,9},{9,8},{12,13},{13,12},{16,17},{17,16... | collective-permute-start | bytes 1966088 | tf_op jit(solution)/shard_map/ppermute | solution.py:44
  5.9 36.0 %collective-permute-start.2 = (bf16[1280,640]{1,0:T(8,128)(2,1)}, bf16[1280,640]{1,0:T(8,128)(2,1)S(1)}, u32[]{:S(2)}, u32[]{:S(2)}) collective-permute-start(bf16[1280,640]{1,0:T(8,128)(2,1)} %refs_2_), channel_id=1, source_target_pairs={{0,12},{1,5},{4,0},{5,9},{8,4},{9,13},{12,8},{13,1},{16,28},{17,21... | collective-permute-start | bytes 4915208 | tf_op jit(solution)/shard_map/ppermute | solution.py:44
  7.2 37.3 %collective-permute-start.1 = (bf16[1280,640]{1,0:T(8,128)(2,1)}, bf16[1280,640]{1,0:T(8,128)(2,1)S(1)}, u32[]{:S(2)}, u32[]{:S(2)}) collective-permute-start(bf16[1280,640]{1,0:T(8,128)(2,1)} %refs_2_), channel_id=1, source_target_pairs={{0,4},{1,13},{4,8},{5,1},{8,12},{9,5},{12,0},{13,9},{16,20},{17,29... | collective-permute-start | bytes 4915208 | tf_op jit(solution)/shard_map/ppermute | solution.py:44
  8.6 39.2 %collective-permute-start.3 = (bf16[1280,640]{1,0:T(8,128)(2,1)}, bf16[1280,640]{1,0:T(8,128)(2,1)}, u32[]{:S(2)}, u32[]{:S(2)}) collective-permute-start(bf16[1280,640]{1,0:T(8,128)(2,1)} %refs_2_), channel_id=1, source_target_pairs={{0,2},{1,3},{4,6},{5,7},{8,10},{9,11},{12,14},{13,15},{16,18},{17,... | collective-permute-start | bytes 4915208 | tf_op jit(solution)/shard_map/ppermute | solution.py:44
  12.8 105.5 %copy-start = (bf16[2,640,512]{2,1,0:T(8,128)(2,1)}, bf16[2,640,512]{2,1,0:T(8,128)(2,1)S(1)}, u32[]{:S(2)}) copy-start(bf16[2,640,512]{2,1,0:T(8,128)(2,1)S(1)} %pad_maximum_fusion.refs_8_.refs_4_) | copy-start | bytes 3932164
  12.8 35.0 %collective-permute-start.5 = (bf16[2,640,512]{2,1,0:T(8,128)(2,1)S(1)}, bf16[2,640,512]{2,1,0:T(8,128)(2,1)S(1)}, u32[]{:S(2)}, u32[]{:S(2)}) collective-permute-start(bf16[2,640,512]{2,1,0:T(8,128)(2,1)S(1)} %pad_maximum_fusion.refs_8_.refs_4_), channel_id=1, source_target_pairs={{0,96},{1,33},{4,100},{5,37},{8,104},{9,41},{12,108},{13,45},{16,1... | collective-permute-start | bytes 3932168 | tf_op jit(solution)/shard_map/ppermute | solution.py:44
  14.5 33.3 %collective-permute-start.4 = (bf16[2,640,512]{2,1,0:T(8,128)(2,1)S(1)}, bf16[2,640,512]{2,1,0:T(8,128)(2,1)S(1)}, u32[]{:S(2)}, u32[]{:S(2)}) collective-permute-start(bf16[2,640,512]{2,1,0:T(8,128)(2,1)S(1)} %pad_maximum_fusion.refs_8_.refs_4_), channel_id=1, source_target_pairs={{0,32},{1,97},{4,36},{5,101},{8,40},{9,105},{12,44},{13,109},{16,4... | collective-permute-start | bytes 3932168 | tf_op jit(solution)/shard_map/ppermute | solution.py:44
  41.9 49.2 %copy-start.4 = (bf16[1280,640]{1,0:T(8,128)(2,1)}, bf16[1280,640]{1,0:T(8,128)(2,1)S(1)}, u32[]{:S(2)}) copy-start(bf16[1280,640]{1,0:T(8,128)(2,1)S(1)} %collective-permute-done.2.refs_4_) | copy-start | bytes 4915204
  44.5 46.5 %copy-start.5 = (bf16[1280,640]{1,0:T(8,128)(2,1)}, bf16[1280,640]{1,0:T(8,128)(2,1)S(1)}, u32[]{:S(2)}) copy-start(bf16[1280,640]{1,0:T(8,128)(2,1)S(1)} %collective-permute-done.1.refs_3_) | copy-start | bytes 4915204
  47.8 41.1 %copy-start.2 = (bf16[2,640,512]{2,1,0:T(8,128)(2,1)}, bf16[2,640,512]{2,1,0:T(8,128)(2,1)S(1)}, u32[]{:S(2)}) copy-start(bf16[2,640,512]{2,1,0:T(8,128)(2,1)S(1)} %collective-permute-done.5.refs_10_.refs_6_) | copy-start | bytes 3932164
  47.8 43.2 %copy-start.3 = (bf16[2,640,512]{2,1,0:T(8,128)(2,1)}, bf16[2,640,512]{2,1,0:T(8,128)(2,1)S(1)}, u32[]{:S(2)}) copy-start(bf16[2,640,512]{2,1,0:T(8,128)(2,1)S(1)} %collective-permute-done.4.refs_9_.refs_5_) | copy-start | bytes 3932164
  47.8 30.4 %collective-permute-start.7 = (bf16[1280,640]{1,0:T(8,128)(2,1)}, bf16[1280,640]{1,0:T(8,128)(2,1)}, u32[]{:S(2)}, u32[]{:S(2)}) collective-permute-start(bf16[1280,640]{1,0:T(8,128)(2,1)} %collective-permute-done.3.refs_6_), channel_id=1, source_target_pairs={{0,4},{1,13},{4,8},{5,1},{8,12},{9,5},{12,0},{13,9},{16,20},{17,29... | collective-permute-start | bytes 4915208 | tf_op jit(solution)/shard_map/ppermute | solution.py:44
  47.9 38.0 %collective-permute-start.6 = (bf16[1280,640]{1,0:T(8,128)(2,1)S(1)}, bf16[1280,640]{1,0:T(8,128)(2,1)S(1)}, u32[]{:S(2)}, u32[]{:S(2)}) collective-permute-start(bf16[1280,640]{1,0:T(8,128)(2,1)S(1)} %collective-permute-done.1.refs_3_), channel_id=1, source_target_pairs={{0,4},{1,13},{4,8},{5,1},{8,12},{9,5},{12,0},{13,9},{16,20},{17,29... | collective-permute-start | bytes 4915208 | tf_op jit(solution)/shard_map/ppermute | solution.py:44
  49.2 29.0 %collective-permute-start.9 = (bf16[2,640,512]{2,1,0:T(8,128)(2,1)S(1)}, bf16[2,640,512]{2,1,0:T(8,128)(2,1)}, u32[]{:S(2)}, u32[]{:S(2)}) collective-permute-start(bf16[2,640,512]{2,1,0:T(8,128)(2,1)S(1)} %pad_maximum_fusion.refs_8_.refs_4_), channel_id=1, source_target_pairs={{0,16},{1,17},{4,20},{5,21},{8,24},{9,25},{12,28},{13,29},{16,0},{... | collective-permute-start | bytes 3932168 | tf_op jit(solution)/shard_map/ppermute | solution.py:44
  50.5 27.8 %collective-permute-start.8 = (bf16[2,640,512]{2,1,0:T(8,128)(2,1)S(1)}, bf16[2,640,512]{2,1,0:T(8,128)(2,1)}, u32[]{:S(2)}, u32[]{:S(2)}) collective-permute-start(bf16[2,640,512]{2,1,0:T(8,128)(2,1)S(1)} %collective-permute-done.4.refs_9_.refs_5_), channel_id=1, source_target_pairs={{0,32},{1,97},{4,36},{5,101},{8,40},{9,105},{12,44},{13,109},{16,4... | collective-permute-start | bytes 3932168 | tf_op jit(solution)/shard_map/ppermute | solution.py:44
  85.9 5.2 %copy-start.6 = (bf16[1280,640]{1,0:T(8,128)(2,1)}, bf16[1280,640]{1,0:T(8,128)(2,1)S(1)}, u32[]{:S(2)}) copy-start(bf16[1280,640]{1,0:T(8,128)(2,1)S(1)} %collective-permute-done.6.refs_5_) | copy-start | bytes 4915204
  85.9 27.6 %collective-permute-start.14 = (bf16[2,640,512]{2,1,0:T(8,128)(2,1)}, bf16[2,640,512]{2,1,0:T(8,128)(2,1)}, u32[]{:S(2)}, u32[]{:S(2)}) collective-permute-start(bf16[2,640,512]{2,1,0:T(8,128)(2,1)} %collective-permute-done.8.refs_11_.refs_7_), channel_id=1, source_target_pairs={{0,16},{1,17},{4,20},{5,21},{8,24},{9,25},{12,28},{13,29},{16,0},{... | collective-permute-start | bytes 3932168 | tf_op jit(solution)/shard_map/ppermute | solution.py:44
  87.3 26.7 %collective-permute-start.13 = (bf16[2,640,512]{2,1,0:T(8,128)(2,1)}, bf16[2,640,512]{2,1,0:T(8,128)(2,1)}, u32[]{:S(2)}, u32[]{:S(2)}) collective-permute-start(bf16[2,640,512]{2,1,0:T(8,128)(2,1)} %collective-permute-done.9.refs_12_.refs_8_), channel_id=1, source_target_pairs={{0,96},{1,33},{4,100},{5,37},{8,104},{9,41},{12,108},{13,45},{16,1... | collective-permute-start | bytes 3932168 | tf_op jit(solution)/shard_map/ppermute | solution.py:44
  88.9 29.4 %collective-permute-start.12 = (bf16[2,640,512]{2,1,0:T(8,128)(2,1)}, bf16[2,640,512]{2,1,0:T(8,128)(2,1)}, u32[]{:S(2)}, u32[]{:S(2)}) collective-permute-start(bf16[2,640,512]{2,1,0:T(8,128)(2,1)} %collective-permute-done.9.refs_12_.refs_8_), channel_id=1, source_target_pairs={{0,32},{1,97},{4,36},{5,101},{8,40},{9,105},{12,44},{13,109},{16,4... | collective-permute-start | bytes 3932168 | tf_op jit(solution)/shard_map/ppermute | solution.py:44
  91.0 44.4 %collective-permute-start.10 = (bf16[1280,640]{1,0:T(8,128)(2,1)}, bf16[1280,640]{1,0:T(8,128)(2,1)S(1)}, u32[]{:S(2)}, u32[]{:S(2)}) collective-permute-start(bf16[1280,640]{1,0:T(8,128)(2,1)} %collective-permute-done.3.refs_6_), channel_id=1, source_target_pairs={{0,12},{1,5},{4,0},{5,9},{8,4},{9,13},{12,8},{13,1},{16,28},{17,21... | collective-permute-start | bytes 4915208 | tf_op jit(solution)/shard_map/ppermute | solution.py:44
  91.1 44.4 %collective-permute-start.11 = (bf16[1280,640]{1,0:T(8,128)(2,1)}, bf16[1280,640]{1,0:T(8,128)(2,1)}, u32[]{:S(2)}, u32[]{:S(2)}) collective-permute-start(bf16[1280,640]{1,0:T(8,128)(2,1)} %collective-permute-done.7.refs_7_), channel_id=1, source_target_pairs={{0,4},{1,13},{4,8},{5,1},{8,12},{9,5},{12,0},{13,9},{16,20},{17,29... | collective-permute-start | bytes 4915208 | tf_op jit(solution)/shard_map/ppermute | solution.py:44
  135.5 1.2 copy-start.1
  143.9 10.1 %collective-permute-start.15 = (f32[1,1280,512]{2,1,0:T(8,128)}, f32[1,1280,512]{2,1,0:T(8,128)S(1)}, u32[]{:S(2)}, u32[]{:S(2)}) collective-permute-start(f32[1,1280,512]{2,1,0:T(8,128)} %shard_map.49), channel_id=1, source_target_pairs={{0,1},{1,0},{4,5},{5,4},{8,9},{9,8},{12,13},{13,12},{16,17},{17,16... | collective-permute-start | bytes 7864328 | tf_op jit(solution)/shard_map/ppermute | solution.py:44

commit v2 on v0

v2 whole, which is shorter than its diff:
```python
import functools

import jax
import jax.numpy as jnp
from jax import lax
from jax.experimental import pallas as pl
from jax.experimental.pallas import tpu as pltpu
from jax.sharding import Mesh, PartitionSpec as P

TILE = 256
AXES = ("z", "ylo", "x", "yhi", "core")
NX, NY, NZ = 4, 4, 4


def flat(z, y, x, c):
    z, y, x = z % NZ, y % NY, x % NX
    return (((z * 2 + y % 2) * NX + x) * 2 + y // 2) * 2 + c


def pairs_of(move):
    return [
        (flat(z, y, x, c), flat(*move(z, y, x, c)))
        for z in range(NZ)
        for y in range(NY)
        for x in range(NX)
        for c in range(2)
    ]


def sign(c):
    return 1 - 2 * c


X_AHEAD = pairs_of(lambda z, y, x, c: (z, y, x + sign(c), c))
X_BACK = pairs_of(lambda z, y, x, c: (z, y, x - sign(c), c))
Z_AHEAD = pairs_of(lambda z, y, x, c: (z + sign(c), y, x, c))
Z_BACK = pairs_of(lambda z, y, x, c: (z - sign(c), y, x, c))
Y_FAR = pairs_of(lambda z, y, x, c: (z, y + 2, x, c))
Y_NEAR = pairs_of(lambda z, y, x, c: (z, y ^ 1, x, c))
SWAP = pairs_of(lambda z, y, x, c: (z, y, x, 1 - c))


def send(value, pairs):
    return lax.ppermute(value, AXES, pairs)


def after(value, *earlier):
    return lax.optimization_barrier((value, *earlier))[0]


CHUNK = TILE // 2


def mask_kernel(meta, own_shape, next_shape, own, following, out, buffer, sems):
    core, first = meta[0], meta[1]
    half = buffer.shape[1]
    rows = pl.ds(pl.multiple_of(core * half, half), half)
    copies = [
        pltpu.make_async_copy(source.at[rows], buffer.at[side], sems.at[side])
        for side, source in enumerate((own, following))
    ]
    for copy in copies:
        copy.start()
    for side, shape in enumerate((own_shape, next_shape)):
        copies[side].wait()
        for i in range(half // CHUNK):
            chunk = pl.ds(i * CHUNK, CHUNK)
            tile_row = first + (core * (half // CHUNK) + i) // 2
            for q in range(shape.shape[0]):
                cols = pl.ds(q * TILE, TILE)
                value = buffer[side, chunk, cols]
                value = jnp.where(shape[q, tile_row] != 0, value, jnp.zeros_like(value))
                out[side, chunk, cols] = value


def masked_half(meta, own_shape, next_shape, own, following):
    half = (own.shape[0] // 2, own.shape[1])
    return pl.pallas_call(
        mask_kernel,
        out_shape=jax.ShapeDtypeStruct((2, *half), own.dtype),
        in_specs=[pl.BlockSpec(memory_space=pltpu.SMEM)] * 3
        + [pl.BlockSpec(memory_space=pltpu.HBM)] * 2,
        out_specs=pl.BlockSpec(memory_space=pltpu.VMEM),
        scratch_shapes=[pltpu.VMEM((2, *half), own.dtype), pltpu.SemaphoreType.DMA((2,))],
        cost_estimate=pl.CostEstimate(flops=0, bytes_accessed=4 * own.size, transcendentals=0),
    )(meta, own_shape, next_shape, own, following)


def block_kernel(spots, b_spots, b_from, plan, sides, has_acc, *refs):
    n_groups, n_sides = len(spots), len(sides)
    n_b = 1 + max(max(pick) for pick in b_from)
    meta, int_shape = refs[:2]
    a_refs = refs[2 : 2 + n_groups]
    b_refs = refs[2 + n_groups : 2 + n_groups + n_b]
    rest = refs[2 + n_groups + n_b :]
    acc_ins = ()
    if has_acc:
        acc_ins, rest = rest[:n_sides], rest[n_sides:]
    outs, rest = rest[:n_sides], rest[n_sides:]
    a_buf, b_buf, acc, a_sem, b_sem, in_sem, out_sem = rest
    depth = a_buf.shape[3]
    row_tiles = int_shape.shape[0]
    strips = ((0, 1), (1, 3), (3, 4), (4, row_tiles))
    window = 2
    followers = {next_pair for _, _, _, next_pair in plan}

    def rows_of(s):
        return pl.ds(strips[s][0] * TILE, (strips[s][1] - strips[s][0]) * TILE)

    def members(pair):
        return (2 * pair, 2 * pair + 1)

    def a_copy(g, s):
        slot, part = plan[g // 2][1], g % 2
        return pltpu.make_async_copy(
            a_refs[g].at[rows_of(s)], a_buf.at[slot, part, rows_of(s)], a_sem.at[slot, part, s]
        )

    def b_copy(j, g, i):
        slot, part = plan[g // 2][1], g % 2
        source = b_refs[b_from[j][sides[i]]]
        if len(source.shape) == 3:
            source = source.at[sides[i]]
        return pltpu.make_async_copy(
            source, b_buf.at[slot, i, pl.ds(part * depth, depth)], b_sem.at[slot, part, i]
        )

    def acc_copy(i, s):
        return pltpu.make_async_copy(
            acc_ins[i].at[rows_of(s)], acc.at[i, rows_of(s)], in_sem.at[i, s]
        )

    def out_copy(i, s):
        return pltpu.make_async_copy(
            acc.at[i, rows_of(s)], outs[i].at[rows_of(s)], out_sem.at[i, s]
        )

    def fetch(pair, s):
        for g in members(pair):
            a_copy(g, s).start()
        if has_acc and pair not in followers:
            for i in range(n_sides):
                acc_copy(i, s).start()

    def begin(pair):
        for g in members(pair):
            for j in range(len(b_spots)):
                @pl.when(meta[b_spots[j]] == meta[spots[g]])
                def _():
                    for i in range(n_sides):
                        b_copy(j, g, i).start()
        for s in range(window):
            fetch(pair, s)

    def guarded(pair, work):
        flag = plan[pair][0]
        if flag is None:
            work()
        else:
            pl.when(meta[1] == flag)(work)

    for pair in range(len(plan)):
        if pair not in followers:
            guarded(pair, functools.partial(begin, pair))

    def multiply(pair):
        _, slot, last, next_pair = plan[pair]
        for g in members(pair):
            for i in range(n_sides):
                b_copy(0, g, i).wait()
        first = [(2 * meta[spots[g]] + meta[0]) * (depth // CHUNK) for g in members(pair)]
        for s in range(len(strips)):
            for g in members(pair):
                a_copy(g, s).wait()
            if has_acc and pair not in followers:
                for i in range(n_sides):
                    acc_copy(i, s).wait()
            if s + window < len(strips):
                fetch(pair, s + window)
            elif s + window == len(strips) and next_pair is not None:
                begin(next_pair)
            for p in range(*strips[s]):
                rows = pl.ds(p * TILE, TILE)
                parts = []
                for h in range(2):
                    for j in range(depth // CHUNK):
                        value = a_buf[slot, h, rows, pl.ds(j * CHUNK, CHUNK)]
                        keep = int_shape[p, (first[h] + j) // 2] != 0
                        parts.append(jnp.where(keep, value, jnp.zeros_like(value)))
                left = jnp.concatenate(parts, axis=1)
                for i in range(n_sides):
                    total = jnp.dot(left, b_buf[slot, i], preferred_element_type=jnp.float32)
                    if has_acc or pair in followers:
                        total = total + acc[i, rows, :]
                    acc[i, rows, :] = total
            if last:
                for i in range(n_sides):
                    out_copy(i, s).start()

    for pair in range(len(plan)):
        guarded(pair, functools.partial(multiply, pair))
    for s in range(len(strips)):
        for i in range(n_sides):
            out_copy(i, s).wait()


def block_matmul(meta, int_shape, groups, b_blocks, sides, plan, weight, accs=()):
    a_refs, spots = [g[0] for g in groups], tuple(g[1] for g in groups)
    b_refs, b_from, b_spots = [], [], []
    for block, spot in b_blocks:
        many = isinstance(block, tuple)
        b_from.append((len(b_refs), len(b_refs) + int(many)))
        b_refs.extend(block if many else (block,))
        b_spots.append(spot)
    rows, depth = a_refs[0].shape
    columns = b_refs[0].shape[-1]
    m = len(sides)
    operands = [meta, int_shape] + a_refs + b_refs + list(accs)
    in_specs = [pl.BlockSpec(memory_space=pltpu.SMEM)] * 2
    in_specs += [pl.BlockSpec(memory_space=pltpu.HBM)] * (len(operands) - 2)
    return pl.pallas_call(
        functools.partial(
            block_kernel, spots, tuple(b_spots), tuple(b_from), plan, sides, bool(accs)
        ),
        out_shape=(jax.ShapeDtypeStruct((rows, columns), jnp.float32),) * m,
        in_specs=in_specs,
        out_specs=(pl.BlockSpec(memory_space=pltpu.HBM),) * m,
        scratch_shapes=[
            pltpu.VMEM((2, 2, rows, depth), jnp.bfloat16),
            pltpu.VMEM((2, m, 2 * depth, columns), jnp.bfloat16),
            pltpu.VMEM((m, rows, columns), jnp.float32),
            pltpu.SemaphoreType.DMA((2, 2, 4)),
            pltpu.SemaphoreType.DMA((2, 2, m)),
            pltpu.SemaphoreType.DMA((m, 4)),
            pltpu.SemaphoreType.DMA((m, 4)),
        ],
        cost_estimate=pl.CostEstimate(
            flops=weight * 2 * rows * depth * columns,
            bytes_accessed=2 * rows * depth,
            transcendentals=0,
        ),
    )(*operands)


def per_device(a, b, int_shape, amp_shape):
    z, ylo, x = lax.axis_index("z"), lax.axis_index("ylo"), lax.axis_index("x")
    yhi, core = lax.axis_index("yhi"), lax.axis_index("core")
    step = sign(core)
    barrier = lax.optimization_barrier

    spots = [x, (x - step) % NX, (x + step) % NX, (x + 2) % NX]
    deep = [z, (z - step) % NZ, (z + step) % NZ, (z + 2) % NZ]
    meta = [core, (ylo == yhi).astype(jnp.int32)]
    meta += [2 * s + yhi for s in spots] + [2 * s + 1 - yhi for s in spots]
    meta += [2 * s + ylo for s in deep] + [2 * s + 1 - ylo for s in deep]
    meta = jnp.stack(meta).astype(jnp.int32)
    first = jnp.stack([core, (2 * z + ylo) * (b.shape[0] // TILE)]).astype(jnp.int32)

    x1 = send(a, X_AHEAD)
    x2 = send(a, X_BACK)
    aq = send(a, Y_FAR)
    shape_t = amp_shape.T
    b0 = masked_half(first, shape_t, send(shape_t, SWAP), b, send(b, SWAP))
    z1 = send(b0, Z_AHEAD)
    z2 = send(b0, Z_BACK)
    x3 = send(x1, X_AHEAD)
    x5 = send(after(aq, x2), X_BACK)
    z3 = send(z1, Z_AHEAD)
    q = send(after(b0, aq, z2), Y_NEAR)
    x4 = send(after(aq, x3), X_AHEAD)
    x6 = send(x5, X_BACK)
    z4 = send(after(q, z3), Z_AHEAD)
    z5 = send(after(q, z3), Z_BACK)
    z6 = send(after(z3, q), Y_NEAR)

    a_blocks = [a, x1, x2, x3, aq, x4, x5, x6]
    groups = [(block, 2 + i) for i, block in enumerate(a_blocks)]
    near = [(block, 10 + i) for i, block in enumerate([b0, z1, z2, z3])]
    far = [(block, 14 + i) for i, block in enumerate([q, z4, z5, z6])]
    ready = groups[:4] + [groups[4], groups[6]]
    near_plan = ((1, 0, False, 1), (1, 1, True, None), (0, 0, True, None))
    far_plan = ((0, 0, False, 1), (0, 1, True, None), (1, 0, True, None))
    sums = block_matmul(meta, int_shape, ready, near, (0, 1), near_plan, 2)
    sums = block_matmul(meta, int_shape, ready, far, (0, 1), far_plan, 6, sums)
    late, late_plan = [groups[5], groups[7]], ((None, 0, True, None),)
    theirs = block_matmul(meta, int_shape, late, near + far, (1,), late_plan, 1, sums[1:])[0]
    got = send(theirs, SWAP)
    ours = block_matmul(meta, int_shape, late, near + far, (0,), late_plan, 1, sums[:1])[0]
    return (ours + got).astype(jnp.bfloat16)


def solution(mesh):
    fine = Mesh(mesh.devices.reshape(NZ, 2, NX, 2, 2), AXES)
    row, col = ("z", "ylo"), ("x", "yhi", "core")
    return jax.shard_map(
        per_device,
        mesh=fine,
        in_specs=(P(row, col), P(row, col), P(row, None), P(None, col)),
        out_specs=P(row, col),
        check_vma=False,
    )
```

time: 411 us -> 139 us (0.34)
  waiting for transfers between devices: 314 us -> 71.9 us
  local copies, waits for them, and re-layouts: 55.8 us -> 2.19 us
  Pallas kernels: 0 us -> 36.3 us
  matrix products: 27 us -> 0 us
  starting transfers between devices: 0.04 us -> 23.7 us
  between operations: 13.4 us -> 0.08 us
    all_gather x2 -> x0, waiting for transfers between devices: 312 us -> none  [the longest x1 157 us: per_device(): left = lax.all_gather(integrals, 'col', axis=1, tiled=True) * int_mask]
    ppermute x0 -> x17, waiting for transfers between devices: none -> 71.9 us  [send(): return lax.ppermute(value, AXES, pairs)]
    pallas_call x0 -> x5, Pallas kernels: none -> 36.3 us  [the longest x4 33.1 us: block_matmul(): pl.pallas_call(functools.partial(block_kernel, spots, tuple(b_spots), tup...]
    unnamed x4 -> x8, local copies, waits for them, and re-layouts: 30.7 us -> 1.57 us
    dot_general x1 -> x0, matrix products: 27 us -> none  [per_device(): total = jnp.dot(left, whole_amp, preferred_element_type=jnp.float32)]
    broadcast_in_dim x4 -> x0, local copies, waits for them, and re-layouts: 25 us -> none  [the longest x2 24.6 us: expand_shape(): jnp.repeat(jnp.repeat(shape_mask, TILE, axis=0), TILE, axis=1)]
    ppermute x0 -> x17, starting transfers between devices: none -> 23.7 us  [send(): return lax.ppermute(value, AXES, pairs)]
  transfers between devices with their start and end apart: 2 -> 17, of which waited for: 2 -> 10; matrix products, arithmetic and copies ran while one was open for 14% -> 1% of each run, Pallas kernels for 0% -> 22%
where the time goes in v2:
time: 139 us; the launch traced here: 138 us
  waiting for transfers between devices  71.9 us (52%)
  Pallas kernels  36.3 us (26%)
  starting transfers between devices  23.7 us (17%)
  other arithmetic  3.85 us (3%)
  local copies, waits for them, and re-layouts  2.19 us (2%)
    ppermute x17, waiting for transfers between devices, send(): return lax.ppermute(value, AXES, pairs)  71.9 us
    pallas_call x4, Pallas kernels, block_matmul(): pl.pallas_call(functools.partial(block_kernel, spots, tuple(b_spots), tup...  33.1 us
    ppermute x17, starting transfers between devices, send(): return lax.ppermute(value, AXES, pairs)  23.7 us
    convert_element_type x1, other arithmetic, per_device(): return (ours + got).astype(jnp.bfloat16)  3.24 us
    pallas_call x1, Pallas kernels, masked_half(): pl.pallas_call(mask_kernel, out_shape=jax.ShapeDtypeStruct((2, *half), ow...  3.16 us
  transfers between devices with their start and end apart: 17, of which 10 were waited for; matrix products, arithmetic and copies ran while one was open for 1% of the time, Pallas kernels for 22%

profile of v2, /device:TPU:1, one launch (start us, length us, event | category | flops | bytes accessed | tf_op | source)
XLA Modules:
  0.0 138.0 jit_solution(15271414758924249021)
XLA Ops:
  0.0 1.4 %collective-permute-start.8 = (bf16[1280,512]{1,0:T(8,128)(2,1)}, bf16[1280,512]{1,0:T(8,128)(2,1)S(1)}, u32[]{:S(2)}, u32[]{:S(2)}) collective-permute-start(bf16[1280,512]{1,0:T(8,128)(2,1)} %own.1), channel_id=1, source_target_pairs={{0,1},{1,0},{4,5},{5,4},{8,9},{9,8},{12,13},{13,12},{16,17},{17,16... | collective-permute-start | bytes 3932168 | tf_op jit(solution)/shard_map/ppermute | solution.py:44
  1.4 2.6 %collective-permute-start.1 = (bf16[1280,640]{1,0:T(8,128)(2,1)}, bf16[1280,640]{1,0:T(8,128)(2,1)}, u32[]{:S(2)}, u32[]{:S(2)}) collective-permute-start(bf16[1280,640]{1,0:T(8,128)(2,1)} %refs_2_.3), channel_id=1, source_target_pairs={{0,4},{1,13},{4,8},{5,1},{8,12},{9,5},{12,0},{13,9},{16,20},{17,29... | collective-permute-start | bytes 4915208 | tf_op jit(solution)/shard_map/ppermute | solution.py:44
  4.0 2.9 %collective-permute-start = (bf16[1280,640]{1,0:T(8,128)(2,1)}, bf16[1280,640]{1,0:T(8,128)(2,1)}, u32[]{:S(2)}, u32[]{:S(2)}) collective-permute-start(bf16[1280,640]{1,0:T(8,128)(2,1)} %refs_2_.3), channel_id=1, source_target_pairs={{0,2},{1,3},{4,6},{5,7},{8,10},{9,11},{12,14},{13,15},{16,18},{17,... | collective-permute-start | bytes 4915208 | tf_op jit(solution)/shard_map/ppermute | solution.py:44
  6.9 1.0 collective-permute-start.7
  7.9 0.6 pad_add_fusion.meta
  9.0 0.5 copy-done.3
  9.5 1.1 copy-done.2
  10.5 3.2 %shard_map.46.refs_8_.refs_4_ = bf16[2,640,512]{2,1,0:T(8,128)(2,1)} custom-call(s32[2]{0:T(128)} %pad_add_fusion.meta, s32[2,40]{1,0:T(2,128)} %bitcast.21, s32[2,40]{1,0:T(2,128)} %copy-done.3, bf16[1280,512]{1,0:T(8,128)(2,1)} %own.1, bf16[1280,512]{1,0:T(8,128)(2,1)} %copy-done.2), custom_call_target="tpu_custom_call" | custom-call | bytes 2621440 | tf_op jit(solution)/shard_map/pallas_call | solution.py:78
  13.7 1.7 %collective-permute-start.10 = (bf16[2,640,512]{2,1,0:T(8,128)(2,1)}, bf16[2,640,512]{2,1,0:T(8,128)(2,1)S(1)}, u32[]{:S(2)}, u32[]{:S(2)}) collective-permute-start(bf16[2,640,512]{2,1,0:T(8,128)(2,1)} %shard_map.46.refs_8_.refs_4_), channel_id=1, source_target_pairs={{0,96},{1,33},{4,100},{5,37},{8,104},{9,41},{12,108},{13,45},{16,1... | collective-permute-start | bytes 3932168 | tf_op jit(solution)/shard_map/ppermute | solution.py:44
  15.4 2.2 %collective-permute-start.9 = (bf16[2,640,512]{2,1,0:T(8,128)(2,1)}, bf16[2,640,512]{2,1,0:T(8,128)(2,1)S(1)}, u32[]{:S(2)}, u32[]{:S(2)}) collective-permute-start(bf16[2,640,512]{2,1,0:T(8,128)(2,1)} %shard_map.46.refs_8_.refs_4_), channel_id=1, source_target_pairs={{0,32},{1,97},{4,36},{5,101},{8,40},{9,105},{12,44},{13,109},{16,4... | collective-permute-start | bytes 3932168 | tf_op jit(solution)/shard_map/ppermute | solution.py:44
  17.6 18.1 %collective-permute-done.1.refs_3_ = bf16[1280,640]{1,0:T(8,128)(2,1)} collective-permute-done((bf16[1280,640]{1,0:T(8,128)(2,1)}, bf16[1280,640]{1,0:T(8,128)(2,1)}, u32[]{:S(2)}, u32[]{:S(2)}) %collective-permute-start.1) | collective-permute-done | bytes 1638432 | tf_op jit(solution)/shard_map/ppermute | solution.py:44
  35.7 3.4 %collective-permute-start.2 = (bf16[1280,640]{1,0:T(8,128)(2,1)}, bf16[1280,640]{1,0:T(8,128)(2,1)}, u32[]{:S(2)}, u32[]{:S(2)}) collective-permute-start(bf16[1280,640]{1,0:T(8,128)(2,1)} %collective-permute-done.1.refs_3_), channel_id=1, source_target_pairs={{0,4},{1,13},{4,8},{5,1},{8,12},{9,5},{12,0},{13,9},{16,20},{17,29... | collective-permute-start | bytes 4915208 | tf_op jit(solution)/shard_map/ppermute | solution.py:44
  39.1 3.7 %collective-permute-done.refs_6_ = bf16[1280,640]{1,0:T(8,128)(2,1)} collective-permute-done((bf16[1280,640]{1,0:T(8,128)(2,1)}, bf16[1280,640]{1,0:T(8,128)(2,1)}, u32[]{:S(2)}, u32[]{:S(2)}) %collective-permute-start) | collective-permute-done | bytes 1638432 | tf_op jit(solution)/shard_map/ppermute | solution.py:44
  42.8 0.6 collective-permute-done.10.refs_10_.refs_6_
  43.4 2.5 %collective-permute-done.9.refs_9_.refs_5_ = bf16[2,640,512]{2,1,0:T(8,128)(2,1)S(1)} collective-permute-done((bf16[2,640,512]{2,1,0:T(8,128)(2,1)}, bf16[2,640,512]{2,1,0:T(8,128)(2,1)S(1)}, u32[]{:S(2)}, u32[]{:S(2)}) %collective-permute-start.9) | collective-permute-done | bytes 1310752 | tf_op jit(solution)/shard_map/ppermute | solution.py:44
  45.9 3.4 %collective-permute-start.11 = (bf16[2,640,512]{2,1,0:T(8,128)(2,1)S(1)}, bf16[2,640,512]{2,1,0:T(8,128)(2,1)}, u32[]{:S(2)}, u32[]{:S(2)}) collective-permute-start(bf16[2,640,512]{2,1,0:T(8,128)(2,1)S(1)} %collective-permute-done.9.refs_9_.refs_5_), channel_id=1, source_target_pairs={{0,32},{1,97},{4,36},{5,101},{8,40},{9,105},{12,44},{13,109},{16,4... | collective-permute-start | bytes 3932168 | tf_op jit(solution)/shard_map/ppermute | solution.py:44
  49.7 14.2 %collective-permute-done.11.refs_11_.refs_7_ = bf16[2,640,512]{2,1,0:T(8,128)(2,1)} collective-permute-done((bf16[2,640,512]{2,1,0:T(8,128)(2,1)S(1)}, bf16[2,640,512]{2,1,0:T(8,128)(2,1)}, u32[]{:S(2)}, u32[]{:S(2)}) %collective-permute-start.11) | collective-permute-done | bytes 1310752 | tf_op jit(solution)/shard_map/ppermute | solution.py:44
  63.8 14.9 %collective-permute-done.12.refs_8_ = bf16[2,640,512]{2,1,0:T(8,128)(2,1)} collective-permute-done((bf16[2,640,512]{2,1,0:T(8,128)(2,1)}, bf16[2,640,512]{2,1,0:T(8,128)(2,1)}, u32[]{:S(2)}, u32[]{:S(2)}) %collective-permute-start.12) | collective-permute-done | bytes 1310752 | tf_op jit(solution)/shard_map/ppermute | solution.py:44
  78.8 0.5 collective-permute-start.13
  79.3 0.9 collective-permute-start.14
  80.2 0.7 collective-permute-start.15
  80.9 1.7 %collective-permute-start.3 = (bf16[1280,640]{1,0:T(8,128)(2,1)}, bf16[1280,640]{1,0:T(8,128)(2,1)}, u32[]{:S(2)}, u32[]{:S(2)}) collective-permute-start(bf16[1280,640]{1,0:T(8,128)(2,1)} %collective-permute-done.refs_6_), channel_id=1, source_target_pairs={{0,4},{1,13},{4,8},{5,1},{8,12},{9,5},{12,0},{13,9},{16,20},{17,29... | collective-permute-start | bytes 4915208 | tf_op jit(solution)/shard_map/ppermute | solution.py:44
  82.6 0.6 stack.86.refs_0_
  83.2 12.2 %shard_map.47 = (f32[1280,512]{1,0:T(8,128)}, f32[1280,512]{1,0:T(8,128)}) custom-call(s32[18]{0:T(128)} %stack.86.refs_0_, s32[5,40]{1,0:T(8,128)} %refs_1_.7, bf16[1280,640]{1,0:T(8,128)(2,1)} %refs_2_.3, bf16[1280,640]{1,0:T(8,128)(2,1)} %collective-permute-done.1.refs_3_, bf16[1280,640]{1,0:T(8,128)(2,1)} %collective-permute-done.4.refs_4_, ...), custom_call_target="tpu_custom_call" | custom-call | flops 1677721600 | bytes 1638400 | tf_op jit(solution)/shard_map/pallas_call | solution.py:221
  95.5 13.6 %collective-permute-done.13.refs_9_ = bf16[2,640,512]{2,1,0:T(8,128)(2,1)} collective-permute-done((bf16[2,640,512]{2,1,0:T(8,128)(2,1)}, bf16[2,640,512]{2,1,0:T(8,128)(2,1)}, u32[]{:S(2)}, u32[]{:S(2)}) %collective-permute-start.13) | collective-permute-done | bytes 1310752 | tf_op jit(solution)/shard_map/ppermute | solution.py:44
  109.1 1.8 %collective-permute-done.14.refs_10_ = bf16[2,640,512]{2,1,0:T(8,128)(2,1)} collective-permute-done((bf16[2,640,512]{2,1,0:T(8,128)(2,1)}, bf16[2,640,512]{2,1,0:T(8,128)(2,1)}, u32[]{:S(2)}, u32[]{:S(2)}) %collective-permute-start.14) | collective-permute-done | bytes 1310752 | tf_op jit(solution)/shard_map/ppermute | solution.py:44
  110.9 8.5 %shard_map.48 = (f32[1280,512]{1,0:T(8,128)}, f32[1280,512]{1,0:T(8,128)}) custom-call(s32[18]{0:T(128)} %stack.86.refs_0_, s32[5,40]{1,0:T(8,128)} %refs_1_.7, bf16[1280,640]{1,0:T(8,128)(2,1)} %refs_2_.3, bf16[1280,640]{1,0:T(8,128)(2,1)} %collective-permute-done.1.refs_3_, bf16[1280,640]{1,0:T(8,128)(2,1)} %collective-permute-done.4.refs_4_, ...), custom_call_target="tpu_custom_call" | custom-call | flops 5033164800 | bytes 1638400 | tf_op jit(solution)/shard_map/pallas_call | solution.py:221
  119.5 2.1 %collective-permute-done.6.refs_3_ = bf16[1280,640]{1,0:T(8,128)(2,1)} collective-permute-done((bf16[1280,640]{1,0:T(8,128)(2,1)}, bf16[1280,640]{1,0:T(8,128)(2,1)}, u32[]{:S(2)}, u32[]{:S(2)}) %collective-permute-start.6) | collective-permute-done | bytes 1638432 | tf_op jit(solution)/shard_map/ppermute | solution.py:44
  121.6 6.2 %shard_map.50 = f32[1280,512]{1,0:T(8,128)} custom-call(s32[18]{0:T(128)} %stack.86.refs_0_, s32[5,40]{1,0:T(8,128)} %refs_1_.7, bf16[1280,640]{1,0:T(8,128)(2,1)} %collective-permute-done.3.refs_2_, bf16[1280,640]{1,0:T(8,128)(2,1)} %collective-permute-done.6.refs_3_, bf16[2,640,512]{2,1,0:T(8,128)(2,1)} %shard_map.46.refs_8_.refs_4_, ...), custom_call_target="tpu_custom_call" | custom-call | flops 838860800 | bytes 1638400 | tf_op jit(solution)/shard_map/pallas_call | solution.py:221
  127.7 0.9 collective-permute-start.16
  128.6 6.2 %shard_map.49 = f32[1280,512]{1,0:T(8,128)} custom-call(s32[18]{0:T(128)} %stack.86.refs_0_, s32[5,40]{1,0:T(8,128)} %refs_1_.7, bf16[1280,640]{1,0:T(8,128)(2,1)} %collective-permute-done.3.refs_2_, bf16[1280,640]{1,0:T(8,128)(2,1)} %collective-permute-done.6.refs_3_, bf16[2,640,512]{2,1,0:T(8,128)(2,1)} %shard_map.46.refs_8_.refs_4_, ...), custom_call_target="tpu_custom_call" | custom-call | flops 838860800 | bytes 1638400 | tf_op jit(solution)/shard_map/pallas_call | solution.py:221
  134.8 3.2 %add_convert_fusion = bf16[1280,512]{1,0:T(8,128)(2,1)} fusion(f32[1280,512]{1,0:T(8,128)} %shard_map.49, f32[1280,512]{1,0:T(8,128)S(1)} %collective-permute-done.16), kind=kLoop, calls=%fused_computation | loop fusion | flops 1310720 | bytes 6553600 | tf_op jit(solution)/shard_map/convert_element_type | solution.py:289
  (18 shorter events, 0.9 us)
Async XLA Ops:
  0.0 9.0 %collective-permute-start.8 = (bf16[1280,512]{1,0:T(8,128)(2,1)}, bf16[1280,512]{1,0:T(8,128)(2,1)S(1)}, u32[]{:S(2)}, u32[]{:S(2)}) collective-permute-start(bf16[1280,512]{1,0:T(8,128)(2,1)} %own.1), channel_id=1, source_target_pairs={{0,1},{1,0},{4,5},{5,4},{8,9},{9,8},{12,13},{13,12},{16,17},{17,16... | collective-permute-start | bytes 3932168 | tf_op jit(solution)/shard_map/ppermute | solution.py:44
  1.4 34.3 %collective-permute-start.1 = (bf16[1280,640]{1,0:T(8,128)(2,1)}, bf16[1280,640]{1,0:T(8,128)(2,1)}, u32[]{:S(2)}, u32[]{:S(2)}) collective-permute-start(bf16[1280,640]{1,0:T(8,128)(2,1)} %refs_2_.3), channel_id=1, source_target_pairs={{0,4},{1,13},{4,8},{5,1},{8,12},{9,5},{12,0},{13,9},{16,20},{17,29... | collective-permute-start | bytes 4915208 | tf_op jit(solution)/shard_map/ppermute | solution.py:44
  4.0 38.8 %collective-permute-start = (bf16[1280,640]{1,0:T(8,128)(2,1)}, bf16[1280,640]{1,0:T(8,128)(2,1)}, u32[]{:S(2)}, u32[]{:S(2)}) collective-permute-start(bf16[1280,640]{1,0:T(8,128)(2,1)} %refs_2_.3), channel_id=1, source_target_pairs={{0,2},{1,3},{4,6},{5,7},{8,10},{9,11},{12,14},{13,15},{16,18},{17,... | collective-permute-start | bytes 4915208 | tf_op jit(solution)/shard_map/ppermute | solution.py:44
  6.9 35.9 %collective-permute-start.4 = (bf16[1280,640]{1,0:T(8,128)(2,1)}, bf16[1280,640]{1,0:T(8,128)(2,1)}, u32[]{:S(2)}, u32[]{:S(2)}) collective-permute-start(bf16[1280,640]{1,0:T(8,128)(2,1)} %refs_2_.3), channel_id=1, source_target_pairs={{0,12},{1,5},{4,0},{5,9},{8,4},{9,13},{12,8},{13,1},{16,28},{17,21... | collective-permute-start | bytes 4915208 | tf_op jit(solution)/shard_map/ppermute | solution.py:44
  6.9 2.1 %collective-permute-start.7 = (s32[2,40]{1,0:T(2,128)}, s32[2,40]{1,0:T(2,128)S(1)}, u32[]{:S(2)}, u32[]{:S(2)}) collective-permute-start(s32[2,40]{1,0:T(2,128)} %bitcast.20), channel_id=1, source_target_pairs={{0,1},{1,0},{4,5},{5,4},{8,9},{9,8},{12,13},{13,12},{16,17},{17,16... | collective-permute-start | bytes 968 | tf_op jit(solution)/shard_map/ppermute | solution.py:44
  9.0 0.5 copy-start.3
  9.5 1.1 copy-start.2
  13.7 29.7 %collective-permute-start.10 = (bf16[2,640,512]{2,1,0:T(8,128)(2,1)}, bf16[2,640,512]{2,1,0:T(8,128)(2,1)S(1)}, u32[]{:S(2)}, u32[]{:S(2)}) collective-permute-start(bf16[2,640,512]{2,1,0:T(8,128)(2,1)} %shard_map.46.refs_8_.refs_4_), channel_id=1, source_target_pairs={{0,96},{1,33},{4,100},{5,37},{8,104},{9,41},{12,108},{13,45},{16,1... | collective-permute-start | bytes 3932168 | tf_op jit(solution)/shard_map/ppermute | solution.py:44
  15.4 30.5 %collective-permute-start.9 = (bf16[2,640,512]{2,1,0:T(8,128)(2,1)}, bf16[2,640,512]{2,1,0:T(8,128)(2,1)S(1)}, u32[]{:S(2)}, u32[]{:S(2)}) collective-permute-start(bf16[2,640,512]{2,1,0:T(8,128)(2,1)} %shard_map.46.refs_8_.refs_4_), channel_id=1, source_target_pairs={{0,32},{1,97},{4,36},{5,101},{8,40},{9,105},{12,44},{13,109},{16,4... | collective-permute-start | bytes 3932168 | tf_op jit(solution)/shard_map/ppermute | solution.py:44
  35.7 45.2 %collective-permute-start.2 = (bf16[1280,640]{1,0:T(8,128)(2,1)}, bf16[1280,640]{1,0:T(8,128)(2,1)}, u32[]{:S(2)}, u32[]{:S(2)}) collective-permute-start(bf16[1280,640]{1,0:T(8,128)(2,1)} %collective-permute-done.1.refs_3_), channel_id=1, source_target_pairs={{0,4},{1,13},{4,8},{5,1},{8,12},{9,5},{12,0},{13,9},{16,20},{17,29... | collective-permute-start | bytes 4915208 | tf_op jit(solution)/shard_map/ppermute | solution.py:44
  42.8 39.8 %collective-permute-start.5 = (bf16[1280,640]{1,0:T(8,128)(2,1)}, bf16[1280,640]{1,0:T(8,128)(2,1)}, u32[]{:S(2)}, u32[]{:S(2)}) collective-permute-start(bf16[1280,640]{1,0:T(8,128)(2,1)} %collective-permute-done.refs_6_), channel_id=1, source_target_pairs={{0,12},{1,5},{4,0},{5,9},{8,4},{9,13},{12,8},{13,1},{16,28},{17,21... | collective-permute-start | bytes 4915208 | tf_op jit(solution)/shard_map/ppermute | solution.py:44
  43.4 39.8 %copy-start = (bf16[2,640,512]{2,1,0:T(8,128)(2,1)}, bf16[2,640,512]{2,1,0:T(8,128)(2,1)S(1)}, u32[]{:S(2)}) copy-start(bf16[2,640,512]{2,1,0:T(8,128)(2,1)S(1)} %collective-permute-done.10.refs_10_.refs_6_) | copy-start | bytes 3932164
  45.9 37.3 %copy-start.1 = (bf16[2,640,512]{2,1,0:T(8,128)(2,1)}, bf16[2,640,512]{2,1,0:T(8,128)(2,1)S(1)}, u32[]{:S(2)}) copy-start(bf16[2,640,512]{2,1,0:T(8,128)(2,1)S(1)} %collective-permute-done.9.refs_9_.refs_5_) | copy-start | bytes 3932164
  45.9 18.0 %collective-permute-start.11 = (bf16[2,640,512]{2,1,0:T(8,128)(2,1)S(1)}, bf16[2,640,512]{2,1,0:T(8,128)(2,1)}, u32[]{:S(2)}, u32[]{:S(2)}) collective-permute-start(bf16[2,640,512]{2,1,0:T(8,128)(2,1)S(1)} %collective-permute-done.9.refs_9_.refs_5_), channel_id=1, source_target_pairs={{0,32},{1,97},{4,36},{5,101},{8,40},{9,105},{12,44},{13,109},{16,4... | collective-permute-start | bytes 3932168 | tf_op jit(solution)/shard_map/ppermute | solution.py:44
  49.3 29.5 %collective-permute-start.12 = (bf16[2,640,512]{2,1,0:T(8,128)(2,1)}, bf16[2,640,512]{2,1,0:T(8,128)(2,1)}, u32[]{:S(2)}, u32[]{:S(2)}) collective-permute-start(bf16[2,640,512]{2,1,0:T(8,128)(2,1)} %shard_map.46.refs_8_.refs_4_), channel_id=1, source_target_pairs={{0,16},{1,17},{4,20},{5,21},{8,24},{9,25},{12,28},{13,29},{16,0},{... | collective-permute-start | bytes 3932168 | tf_op jit(solution)/shard_map/ppermute | solution.py:44
  78.8 30.3 %collective-permute-start.13 = (bf16[2,640,512]{2,1,0:T(8,128)(2,1)}, bf16[2,640,512]{2,1,0:T(8,128)(2,1)}, u32[]{:S(2)}, u32[]{:S(2)}) collective-permute-start(bf16[2,640,512]{2,1,0:T(8,128)(2,1)} %collective-permute-done.12.refs_8_), channel_id=1, source_target_pairs={{0,32},{1,97},{4,36},{5,101},{8,40},{9,105},{12,44},{13,109},{16,4... | collective-permute-start | bytes 3932168 | tf_op jit(solution)/shard_map/ppermute | solution.py:44
  79.3 31.6 %collective-permute-start.14 = (bf16[2,640,512]{2,1,0:T(8,128)(2,1)}, bf16[2,640,512]{2,1,0:T(8,128)(2,1)}, u32[]{:S(2)}, u32[]{:S(2)}) collective-permute-start(bf16[2,640,512]{2,1,0:T(8,128)(2,1)} %collective-permute-done.12.refs_8_), channel_id=1, source_target_pairs={{0,96},{1,33},{4,100},{5,37},{8,104},{9,41},{12,108},{13,45},{16,1... | collective-permute-start | bytes 3932168 | tf_op jit(solution)/shard_map/ppermute | solution.py:44
  80.2 30.7 %collective-permute-start.15 = (bf16[2,640,512]{2,1,0:T(8,128)(2,1)}, bf16[2,640,512]{2,1,0:T(8,128)(2,1)}, u32[]{:S(2)}, u32[]{:S(2)}) collective-permute-start(bf16[2,640,512]{2,1,0:T(8,128)(2,1)} %collective-permute-done.11.refs_11_.refs_7_), channel_id=1, source_target_pairs={{0,16},{1,17},{4,20},{5,21},{8,24},{9,25},{12,28},{13,29},{16,0},{... | collective-permute-start | bytes 3932168 | tf_op jit(solution)/shard_map/ppermute | solution.py:44
  80.9 38.5 %collective-permute-start.3 = (bf16[1280,640]{1,0:T(8,128)(2,1)}, bf16[1280,640]{1,0:T(8,128)(2,1)}, u32[]{:S(2)}, u32[]{:S(2)}) collective-permute-start(bf16[1280,640]{1,0:T(8,128)(2,1)} %collective-permute-done.refs_6_), channel_id=1, source_target_pairs={{0,4},{1,13},{4,8},{5,1},{8,12},{9,5},{12,0},{13,9},{16,20},{17,29... | collective-permute-start | bytes 4915208 | tf_op jit(solution)/shard_map/ppermute | solution.py:44
  82.6 39.0 %collective-permute-start.6 = (bf16[1280,640]{1,0:T(8,128)(2,1)}, bf16[1280,640]{1,0:T(8,128)(2,1)}, u32[]{:S(2)}, u32[]{:S(2)}) collective-permute-start(bf16[1280,640]{1,0:T(8,128)(2,1)} %collective-permute-done.5.refs_7_), channel_id=1, source_target_pairs={{0,12},{1,5},{4,0},{5,9},{8,4},{9,13},{12,8},{13,1},{16,28},{17,21... | collective-permute-start | bytes 4915208 | tf_op jit(solution)/shard_map/ppermute | solution.py:44
  127.7 7.0 %collective-permute-start.16 = (f32[1280,512]{1,0:T(8,128)}, f32[1280,512]{1,0:T(8,128)S(1)}, u32[]{:S(2)}, u32[]{:S(2)}) collective-permute-start(f32[1280,512]{1,0:T(8,128)} %shard_map.50), channel_id=1, source_target_pairs={{0,1},{1,0},{4,5},{5,4},{8,9},{9,8},{12,13},{13,12},{16,17},{17,16... | collective-permute-start | bytes 7864328 | tf_op jit(solution)/shard_map/ppermute | solution.py:44

commit v3 on v2

--- a/solution.py
+++ b/solution.py
@@ -263,10 +263,10 @@
     b0 = masked_half(first, shape_t, send(shape_t, SWAP), b, send(b, SWAP))
     z1 = send(b0, Z_AHEAD)
     z2 = send(b0, Z_BACK)
+    q = send(after(b0, x1), Y_NEAR)
     x3 = send(x1, X_AHEAD)
     x5 = send(after(aq, x2), X_BACK)
-    z3 = send(z1, Z_AHEAD)
-    q = send(after(b0, aq, z2), Y_NEAR)
+    z3 = send(after(z1, z2), Z_AHEAD)
     x4 = send(after(aq, x3), X_AHEAD)
     x6 = send(x5, X_BACK)
     z4 = send(after(q, z3), Z_AHEAD)
@@ -281,7 +281,7 @@
     near_plan = ((1, 0, False, 1), (1, 1, True, None), (0, 0, True, None))
     far_plan = ((0, 0, False, 1), (0, 1, True, None), (1, 0, True, None))
     sums = block_matmul(meta, int_shape, ready, near, (0, 1), near_plan, 2)
-    sums = block_matmul(meta, int_shape, ready, far, (0, 1), far_plan, 6, sums)
+    sums = block_matmul(meta, int_shape, ready, far, (0, 1), far_plan, 7, sums)
     late, late_plan = [groups[5], groups[7]], ((None, 0, True, None),)
     theirs = block_matmul(meta, int_shape, late, near + far, (1,), late_plan, 1, sums[1:])[0]
     got = send(theirs, SWAP)

time: 139 us -> 138 us (level); the launches traced: 138 us -> 135 us
  waiting for transfers between devices: 71.9 us -> 62.6 us
  starting transfers between devices: 23.7 us -> 30.5 us
    ppermute x17, waiting for transfers between devices: 71.9 us -> 62.6 us  [send(): return lax.ppermute(value, AXES, pairs)]
    ppermute x17, starting transfers between devices: 23.7 us -> 30.5 us  [send(): return lax.ppermute(value, AXES, pairs)]
  transfers between devices with their start and end apart: 17 -> 17, of which waited for: 10 -> 8; matrix products, arithmetic and copies ran while one was open for 1% -> 1% of each run, Pallas kernels for 22% -> 22%
where the time goes in v3:
time: 138 us; the launch traced here: 135 us
  waiting for transfers between devices  62.6 us (45%)
  Pallas kernels  36.3 us (26%)
  starting transfers between devices  30.5 us (22%)
  other arithmetic  3.85 us (3%)
  local copies, waits for them, and re-layouts  2.19 us (2%)
    ppermute x17, waiting for transfers between devices, send(): return lax.ppermute(value, AXES, pairs)  62.6 us
    pallas_call x4, Pallas kernels, block_matmul(): pl.pallas_call(functools.partial(block_kernel, spots, tuple(b_spots), tup...  33.1 us
    ppermute x17, starting transfers between devices, send(): return lax.ppermute(value, AXES, pairs)  30.5 us
    convert_element_type x1, other arithmetic, per_device(): return (ours + got).astype(jnp.bfloat16)  3.24 us
    pallas_call x1, Pallas kernels, masked_half(): pl.pallas_call(mask_kernel, out_shape=jax.ShapeDtypeStruct((2, *half), ow...  3.16 us
  transfers between devices with their start and end apart: 17, of which 8 were waited for; matrix products, arithmetic and copies ran while one was open for 1% of the time, Pallas kernels for 22%

profile of v3, /device:TPU:1, one launch (start us, length us, event | category | flops | bytes accessed | tf_op | source)
XLA Modules:
  0.0 135.5 jit_solution(14508778410680278370)
XLA Ops:
  0.0 1.4 %collective-permute-start.8 = (bf16[1280,512]{1,0:T(8,128)(2,1)}, bf16[1280,512]{1,0:T(8,128)(2,1)S(1)}, u32[]{:S(2)}, u32[]{:S(2)}) collective-permute-start(bf16[1280,512]{1,0:T(8,128)(2,1)} %own.1), channel_id=1, source_target_pairs={{0,1},{1,0},{4,5},{5,4},{8,9},{9,8},{12,13},{13,12},{16,17},{17,16... | collective-permute-start | bytes 3932168 | tf_op jit(solution)/shard_map/ppermute | solution.py:44
  1.4 2.6 %collective-permute-start.1 = (bf16[1280,640]{1,0:T(8,128)(2,1)}, bf16[1280,640]{1,0:T(8,128)(2,1)}, u32[]{:S(2)}, u32[]{:S(2)}) collective-permute-start(bf16[1280,640]{1,0:T(8,128)(2,1)} %refs_2_.3), channel_id=1, source_target_pairs={{0,4},{1,13},{4,8},{5,1},{8,12},{9,5},{12,0},{13,9},{16,20},{17,29... | collective-permute-start | bytes 4915208 | tf_op jit(solution)/shard_map/ppermute | solution.py:44
  4.0 2.9 %collective-permute-start = (bf16[1280,640]{1,0:T(8,128)(2,1)}, bf16[1280,640]{1,0:T(8,128)(2,1)}, u32[]{:S(2)}, u32[]{:S(2)}) collective-permute-start(bf16[1280,640]{1,0:T(8,128)(2,1)} %refs_2_.3), channel_id=1, source_target_pairs={{0,2},{1,3},{4,6},{5,7},{8,10},{9,11},{12,14},{13,15},{16,18},{17,... | collective-permute-start | bytes 4915208 | tf_op jit(solution)/shard_map/ppermute | solution.py:44
  6.9 0.0 collective-permute-start.4
  6.9 1.0 collective-permute-start.7
  7.9 0.6 pad_add_fusion.meta
  8.6 0.4 collective-permute-done.7.next_shape
  9.0 0.5 copy-done.3
  9.5 1.1 copy-done.2
  10.5 3.2 %shard_map.46.refs_8_.refs_4_ = bf16[2,640,512]{2,1,0:T(8,128)(2,1)} custom-call(s32[2]{0:T(128)} %pad_add_fusion.meta, s32[2,40]{1,0:T(2,128)} %bitcast.21, s32[2,40]{1,0:T(2,128)} %copy-done.3, bf16[1280,512]{1,0:T(8,128)(2,1)} %own.1, bf16[1280,512]{1,0:T(8,128)(2,1)} %copy-done.2), custom_call_target="tpu_custom_call" | custom-call | bytes 2621440 | tf_op jit(solution)/shard_map/pallas_call | solution.py:78
  13.7 1.7 %collective-permute-start.10 = (bf16[2,640,512]{2,1,0:T(8,128)(2,1)}, bf16[2,640,512]{2,1,0:T(8,128)(2,1)S(1)}, u32[]{:S(2)}, u32[]{:S(2)}) collective-permute-start(bf16[2,640,512]{2,1,0:T(8,128)(2,1)} %shard_map.46.refs_8_.refs_4_), channel_id=1, source_target_pairs={{0,96},{1,33},{4,100},{5,37},{8,104},{9,41},{12,108},{13,45},{16,1... | collective-permute-start | bytes 3932168 | tf_op jit(solution)/shard_map/ppermute | solution.py:44
  15.4 2.2 %collective-permute-start.9 = (bf16[2,640,512]{2,1,0:T(8,128)(2,1)}, bf16[2,640,512]{2,1,0:T(8,128)(2,1)S(1)}, u32[]{:S(2)}, u32[]{:S(2)}) collective-permute-start(bf16[2,640,512]{2,1,0:T(8,128)(2,1)} %shard_map.46.refs_8_.refs_4_), channel_id=1, source_target_pairs={{0,32},{1,97},{4,36},{5,101},{8,40},{9,105},{12,44},{13,109},{16,4... | collective-permute-start | bytes 3932168 | tf_op jit(solution)/shard_map/ppermute | solution.py:44
  17.6 18.1 %collective-permute-done.1.refs_3_ = bf16[1280,640]{1,0:T(8,128)(2,1)} collective-permute-done((bf16[1280,640]{1,0:T(8,128)(2,1)}, bf16[1280,640]{1,0:T(8,128)(2,1)}, u32[]{:S(2)}, u32[]{:S(2)}) %collective-permute-start.1) | collective-permute-done | bytes 1638432 | tf_op jit(solution)/shard_map/ppermute | solution.py:44
  35.7 3.4 %collective-permute-start.2 = (bf16[1280,640]{1,0:T(8,128)(2,1)}, bf16[1280,640]{1,0:T(8,128)(2,1)}, u32[]{:S(2)}, u32[]{:S(2)}) collective-permute-start(bf16[1280,640]{1,0:T(8,128)(2,1)} %collective-permute-done.1.refs_3_), channel_id=1, source_target_pairs={{0,4},{1,13},{4,8},{5,1},{8,12},{9,5},{12,0},{13,9},{16,20},{17,29... | collective-permute-start | bytes 4915208 | tf_op jit(solution)/shard_map/ppermute | solution.py:44
  39.1 3.7 %collective-permute-done.refs_6_ = bf16[1280,640]{1,0:T(8,128)(2,1)} collective-permute-done((bf16[1280,640]{1,0:T(8,128)(2,1)}, bf16[1280,640]{1,0:T(8,128)(2,1)}, u32[]{:S(2)}, u32[]{:S(2)}) %collective-permute-start) | collective-permute-done | bytes 1638432 | tf_op jit(solution)/shard_map/ppermute | solution.py:44
  42.8 1.6 %collective-permute-start.12 = (bf16[2,640,512]{2,1,0:T(8,128)(2,1)}, bf16[2,640,512]{2,1,0:T(8,128)(2,1)}, u32[]{:S(2)}, u32[]{:S(2)}) collective-permute-start(bf16[2,640,512]{2,1,0:T(8,128)(2,1)} %shard_map.46.refs_8_.refs_4_), channel_id=1, source_target_pairs={{0,16},{1,17},{4,20},{5,21},{8,24},{9,25},{12,28},{13,29},{16,0},{... | collective-permute-start | bytes 3932168 | tf_op jit(solution)/shard_map/ppermute | solution.py:44
  44.4 1.5 %collective-permute-done.9.refs_9_.refs_5_ = bf16[2,640,512]{2,1,0:T(8,128)(2,1)S(1)} collective-permute-done((bf16[2,640,512]{2,1,0:T(8,128)(2,1)}, bf16[2,640,512]{2,1,0:T(8,128)(2,1)S(1)}, u32[]{:S(2)}, u32[]{:S(2)}) %collective-permute-start.9) | collective-permute-done | bytes 1310752 | tf_op jit(solution)/shard_map/ppermute | solution.py:44
  45.9 3.4 %collective-permute-start.11 = (bf16[2,640,512]{2,1,0:T(8,128)(2,1)S(1)}, bf16[2,640,512]{2,1,0:T(8,128)(2,1)}, u32[]{:S(2)}, u32[]{:S(2)}) collective-permute-start(bf16[2,640,512]{2,1,0:T(8,128)(2,1)S(1)} %collective-permute-done.9.refs_9_.refs_5_), channel_id=1, source_target_pairs={{0,32},{1,97},{4,36},{5,101},{8,40},{9,105},{12,44},{13,109},{16,4... | collective-permute-start | bytes 3932168 | tf_op jit(solution)/shard_map/ppermute | solution.py:44
  49.3 22.3 %collective-permute-done.12.refs_8_ = bf16[2,640,512]{2,1,0:T(8,128)(2,1)} collective-permute-done((bf16[2,640,512]{2,1,0:T(8,128)(2,1)}, bf16[2,640,512]{2,1,0:T(8,128)(2,1)}, u32[]{:S(2)}, u32[]{:S(2)}) %collective-permute-start.12) | collective-permute-done | bytes 1310752 | tf_op jit(solution)/shard_map/ppermute | solution.py:44
  71.6 3.8 %collective-permute-start.13 = (bf16[2,640,512]{2,1,0:T(8,128)(2,1)}, bf16[2,640,512]{2,1,0:T(8,128)(2,1)}, u32[]{:S(2)}, u32[]{:S(2)}) collective-permute-start(bf16[2,640,512]{2,1,0:T(8,128)(2,1)} %collective-permute-done.12.refs_8_), channel_id=1, source_target_pairs={{0,32},{1,97},{4,36},{5,101},{8,40},{9,105},{12,44},{13,109},{16,4... | collective-permute-start | bytes 3932168 | tf_op jit(solution)/shard_map/ppermute | solution.py:44
  75.4 1.6 %collective-permute-start.15 = (bf16[2,640,512]{2,1,0:T(8,128)(2,1)}, bf16[2,640,512]{2,1,0:T(8,128)(2,1)}, u32[]{:S(2)}, u32[]{:S(2)}) collective-permute-start(bf16[2,640,512]{2,1,0:T(8,128)(2,1)} %collective-permute-done.11.refs_11_.refs_7_), channel_id=1, source_target_pairs={{0,16},{1,17},{4,20},{5,21},{8,24},{9,25},{12,28},{13,29},{16,0},{... | collective-permute-start | bytes 3932168 | tf_op jit(solution)/shard_map/ppermute | solution.py:44
  77.0 4.7 %collective-permute-start.3 = (bf16[1280,640]{1,0:T(8,128)(2,1)}, bf16[1280,640]{1,0:T(8,128)(2,1)}, u32[]{:S(2)}, u32[]{:S(2)}) collective-permute-start(bf16[1280,640]{1,0:T(8,128)(2,1)} %collective-permute-done.refs_6_), channel_id=1, source_target_pairs={{0,4},{1,13},{4,8},{5,1},{8,12},{9,5},{12,0},{13,9},{16,20},{17,29... | collective-permute-start | bytes 4915208 | tf_op jit(solution)/shard_map/ppermute | solution.py:44
  81.8 0.6 stack.86.refs_0_
  82.4 12.2 %shard_map.47 = (f32[1280,512]{1,0:T(8,128)}, f32[1280,512]{1,0:T(8,128)}) custom-call(s32[18]{0:T(128)} %stack.86.refs_0_, s32[5,40]{1,0:T(8,128)} %refs_1_.7, bf16[1280,640]{1,0:T(8,128)(2,1)} %refs_2_.3, bf16[1280,640]{1,0:T(8,128)(2,1)} %collective-permute-done.1.refs_3_, bf16[1280,640]{1,0:T(8,128)(2,1)} %collective-permute-done.4.refs_4_, ...), custom_call_target="tpu_custom_call" | custom-call | flops 1677721600 | bytes 1638400 | tf_op jit(solution)/shard_map/pallas_call | solution.py:221
  94.6 6.3 %collective-permute-done.13.refs_9_ = bf16[2,640,512]{2,1,0:T(8,128)(2,1)} collective-permute-done((bf16[2,640,512]{2,1,0:T(8,128)(2,1)}, bf16[2,640,512]{2,1,0:T(8,128)(2,1)}, u32[]{:S(2)}, u32[]{:S(2)}) %collective-permute-start.13) | collective-permute-done | bytes 1310752 | tf_op jit(solution)/shard_map/ppermute | solution.py:44
  100.9 6.5 %collective-permute-done.14.refs_10_ = bf16[2,640,512]{2,1,0:T(8,128)(2,1)} collective-permute-done((bf16[2,640,512]{2,1,0:T(8,128)(2,1)}, bf16[2,640,512]{2,1,0:T(8,128)(2,1)}, u32[]{:S(2)}, u32[]{:S(2)}) %collective-permute-start.14) | collective-permute-done | bytes 1310752 | tf_op jit(solution)/shard_map/ppermute | solution.py:44
  107.4 8.5 %shard_map.48 = (f32[1280,512]{1,0:T(8,128)}, f32[1280,512]{1,0:T(8,128)}) custom-call(s32[18]{0:T(128)} %stack.86.refs_0_, s32[5,40]{1,0:T(8,128)} %refs_1_.7, bf16[1280,640]{1,0:T(8,128)(2,1)} %refs_2_.3, bf16[1280,640]{1,0:T(8,128)(2,1)} %collective-permute-done.1.refs_3_, bf16[1280,640]{1,0:T(8,128)(2,1)} %collective-permute-done.4.refs_4_, ...), custom_call_target="tpu_custom_call" | custom-call | flops 5872025600 | bytes 1638400 | tf_op jit(solution)/shard_map/pallas_call | solution.py:221
  116.0 3.8 %collective-permute-done.6.refs_3_ = bf16[1280,640]{1,0:T(8,128)(2,1)} collective-permute-done((bf16[1280,640]{1,0:T(8,128)(2,1)}, bf16[1280,640]{1,0:T(8,128)(2,1)}, u32[]{:S(2)}, u32[]{:S(2)}) %collective-permute-start.6) | collective-permute-done | bytes 1638432 | tf_op jit(solution)/shard_map/ppermute | solution.py:44
  119.8 6.2 %shard_map.50 = f32[1280,512]{1,0:T(8,128)} custom-call(s32[18]{0:T(128)} %stack.86.refs_0_, s32[5,40]{1,0:T(8,128)} %refs_1_.7, bf16[1280,640]{1,0:T(8,128)(2,1)} %collective-permute-done.3.refs_2_, bf16[1280,640]{1,0:T(8,128)(2,1)} %collective-permute-done.6.refs_3_, bf16[2,640,512]{2,1,0:T(8,128)(2,1)} %shard_map.46.refs_8_.refs_4_, ...), custom_call_target="tpu_custom_call" | custom-call | flops 838860800 | bytes 1638400 | tf_op jit(solution)/shard_map/pallas_call | solution.py:221
  125.9 0.1 collective-permute-start.16
  126.0 6.2 %shard_map.49 = f32[1280,512]{1,0:T(8,128)} custom-call(s32[18]{0:T(128)} %stack.86.refs_0_, s32[5,40]{1,0:T(8,128)} %refs_1_.7, bf16[1280,640]{1,0:T(8,128)(2,1)} %collective-permute-done.3.refs_2_, bf16[1280,640]{1,0:T(8,128)(2,1)} %collective-permute-done.6.refs_3_, bf16[2,640,512]{2,1,0:T(8,128)(2,1)} %shard_map.46.refs_8_.refs_4_, ...), custom_call_target="tpu_custom_call" | custom-call | flops 838860800 | bytes 1638400 | tf_op jit(solution)/shard_map/pallas_call | solution.py:221
  132.2 3.2 %add_convert_fusion = bf16[1280,512]{1,0:T(8,128)(2,1)} fusion(f32[1280,512]{1,0:T(8,128)} %shard_map.49, f32[1280,512]{1,0:T(8,128)S(1)} %collective-permute-done.16), kind=kLoop, calls=%fused_computation | loop fusion | flops 1310720 | bytes 6553600 | tf_op jit(solution)/shard_map/convert_element_type | solution.py:289
  (18 shorter events, 0.0 us)
Async XLA Ops:
  0.0 9.0 %collective-permute-start.8 = (bf16[1280,512]{1,0:T(8,128)(2,1)}, bf16[1280,512]{1,0:T(8,128)(2,1)S(1)}, u32[]{:S(2)}, u32[]{:S(2)}) collective-permute-start(bf16[1280,512]{1,0:T(8,128)(2,1)} %own.1), channel_id=1, source_target_pairs={{0,1},{1,0},{4,5},{5,4},{8,9},{9,8},{12,13},{13,12},{16,17},{17,16... | collective-permute-start | bytes 3932168 | tf_op jit(solution)/shard_map/ppermute | solution.py:44
  1.4 34.3 %collective-permute-start.1 = (bf16[1280,640]{1,0:T(8,128)(2,1)}, bf16[1280,640]{1,0:T(8,128)(2,1)}, u32[]{:S(2)}, u32[]{:S(2)}) collective-permute-start(bf16[1280,640]{1,0:T(8,128)(2,1)} %refs_2_.3), channel_id=1, source_target_pairs={{0,4},{1,13},{4,8},{5,1},{8,12},{9,5},{12,0},{13,9},{16,20},{17,29... | collective-permute-start | bytes 4915208 | tf_op jit(solution)/shard_map/ppermute | solution.py:44
  4.0 38.8 %collective-permute-start = (bf16[1280,640]{1,0:T(8,128)(2,1)}, bf16[1280,640]{1,0:T(8,128)(2,1)}, u32[]{:S(2)}, u32[]{:S(2)}) collective-permute-start(bf16[1280,640]{1,0:T(8,128)(2,1)} %refs_2_.3), channel_id=1, source_target_pairs={{0,2},{1,3},{4,6},{5,7},{8,10},{9,11},{12,14},{13,15},{16,18},{17,... | collective-permute-start | bytes 4915208 | tf_op jit(solution)/shard_map/ppermute | solution.py:44
  6.9 35.9 %collective-permute-start.4 = (bf16[1280,640]{1,0:T(8,128)(2,1)}, bf16[1280,640]{1,0:T(8,128)(2,1)}, u32[]{:S(2)}, u32[]{:S(2)}) collective-permute-start(bf16[1280,640]{1,0:T(8,128)(2,1)} %refs_2_.3), channel_id=1, source_target_pairs={{0,12},{1,5},{4,0},{5,9},{8,4},{9,13},{12,8},{13,1},{16,28},{17,21... | collective-permute-start | bytes 4915208 | tf_op jit(solution)/shard_map/ppermute | solution.py:44
  6.9 2.1 %collective-permute-start.7 = (s32[2,40]{1,0:T(2,128)}, s32[2,40]{1,0:T(2,128)S(1)}, u32[]{:S(2)}, u32[]{:S(2)}) collective-permute-start(s32[2,40]{1,0:T(2,128)} %bitcast.20), channel_id=1, source_target_pairs={{0,1},{1,0},{4,5},{5,4},{8,9},{9,8},{12,13},{13,12},{16,17},{17,16... | collective-permute-start | bytes 968 | tf_op jit(solution)/shard_map/ppermute | solution.py:44
  9.0 0.5 copy-start.3
  9.5 1.1 copy-start.2
  13.7 30.7 %collective-permute-start.10 = (bf16[2,640,512]{2,1,0:T(8,128)(2,1)}, bf16[2,640,512]{2,1,0:T(8,128)(2,1)S(1)}, u32[]{:S(2)}, u32[]{:S(2)}) collective-permute-start(bf16[2,640,512]{2,1,0:T(8,128)(2,1)} %shard_map.46.refs_8_.refs_4_), channel_id=1, source_target_pairs={{0,96},{1,33},{4,100},{5,37},{8,104},{9,41},{12,108},{13,45},{16,1... | collective-permute-start | bytes 3932168 | tf_op jit(solution)/shard_map/ppermute | solution.py:44
  15.4 30.5 %collective-permute-start.9 = (bf16[2,640,512]{2,1,0:T(8,128)(2,1)}, bf16[2,640,512]{2,1,0:T(8,128)(2,1)S(1)}, u32[]{:S(2)}, u32[]{:S(2)}) collective-permute-start(bf16[2,640,512]{2,1,0:T(8,128)(2,1)} %shard_map.46.refs_8_.refs_4_), channel_id=1, source_target_pairs={{0,32},{1,97},{4,36},{5,101},{8,40},{9,105},{12,44},{13,109},{16,4... | collective-permute-start | bytes 3932168 | tf_op jit(solution)/shard_map/ppermute | solution.py:44
  35.7 41.3 %collective-permute-start.2 = (bf16[1280,640]{1,0:T(8,128)(2,1)}, bf16[1280,640]{1,0:T(8,128)(2,1)}, u32[]{:S(2)}, u32[]{:S(2)}) collective-permute-start(bf16[1280,640]{1,0:T(8,128)(2,1)} %collective-permute-done.1.refs_3_), channel_id=1, source_target_pairs={{0,4},{1,13},{4,8},{5,1},{8,12},{9,5},{12,0},{13,9},{16,20},{17,29... | collective-permute-start | bytes 4915208 | tf_op jit(solution)/shard_map/ppermute | solution.py:44
  42.8 38.9 %collective-permute-start.5 = (bf16[1280,640]{1,0:T(8,128)(2,1)}, bf16[1280,640]{1,0:T(8,128)(2,1)}, u32[]{:S(2)}, u32[]{:S(2)}) collective-permute-start(bf16[1280,640]{1,0:T(8,128)(2,1)} %collective-permute-done.refs_6_), channel_id=1, source_target_pairs={{0,12},{1,5},{4,0},{5,9},{8,4},{9,13},{12,8},{13,1},{16,28},{17,21... | collective-permute-start | bytes 4915208 | tf_op jit(solution)/shard_map/ppermute | solution.py:44
  42.8 28.8 %collective-permute-start.12 = (bf16[2,640,512]{2,1,0:T(8,128)(2,1)}, bf16[2,640,512]{2,1,0:T(8,128)(2,1)}, u32[]{:S(2)}, u32[]{:S(2)}) collective-permute-start(bf16[2,640,512]{2,1,0:T(8,128)(2,1)} %shard_map.46.refs_8_.refs_4_), channel_id=1, source_target_pairs={{0,16},{1,17},{4,20},{5,21},{8,24},{9,25},{12,28},{13,29},{16,0},{... | collective-permute-start | bytes 3932168 | tf_op jit(solution)/shard_map/ppermute | solution.py:44
  44.4 38.0 %copy-start = (bf16[2,640,512]{2,1,0:T(8,128)(2,1)}, bf16[2,640,512]{2,1,0:T(8,128)(2,1)S(1)}, u32[]{:S(2)}) copy-start(bf16[2,640,512]{2,1,0:T(8,128)(2,1)S(1)} %collective-permute-done.10.refs_10_.refs_6_) | copy-start | bytes 3932164
  45.9 36.5 %copy-start.1 = (bf16[2,640,512]{2,1,0:T(8,128)(2,1)}, bf16[2,640,512]{2,1,0:T(8,128)(2,1)S(1)}, u32[]{:S(2)}) copy-start(bf16[2,640,512]{2,1,0:T(8,128)(2,1)S(1)} %collective-permute-done.9.refs_9_.refs_5_) | copy-start | bytes 3932164
  45.9 25.7 %collective-permute-start.11 = (bf16[2,640,512]{2,1,0:T(8,128)(2,1)S(1)}, bf16[2,640,512]{2,1,0:T(8,128)(2,1)}, u32[]{:S(2)}, u32[]{:S(2)}) collective-permute-start(bf16[2,640,512]{2,1,0:T(8,128)(2,1)S(1)} %collective-permute-done.9.refs_9_.refs_5_), channel_id=1, source_target_pairs={{0,32},{1,97},{4,36},{5,101},{8,40},{9,105},{12,44},{13,109},{16,4... | collective-permute-start | bytes 3932168 | tf_op jit(solution)/shard_map/ppermute | solution.py:44
  71.6 29.3 %collective-permute-start.13 = (bf16[2,640,512]{2,1,0:T(8,128)(2,1)}, bf16[2,640,512]{2,1,0:T(8,128)(2,1)}, u32[]{:S(2)}, u32[]{:S(2)}) collective-permute-start(bf16[2,640,512]{2,1,0:T(8,128)(2,1)} %collective-permute-done.12.refs_8_), channel_id=1, source_target_pairs={{0,32},{1,97},{4,36},{5,101},{8,40},{9,105},{12,44},{13,109},{16,4... | collective-permute-start | bytes 3932168 | tf_op jit(solution)/shard_map/ppermute | solution.py:44
  75.4 32.1 %collective-permute-start.14 = (bf16[2,640,512]{2,1,0:T(8,128)(2,1)}, bf16[2,640,512]{2,1,0:T(8,128)(2,1)}, u32[]{:S(2)}, u32[]{:S(2)}) collective-permute-start(bf16[2,640,512]{2,1,0:T(8,128)(2,1)} %collective-permute-done.12.refs_8_), channel_id=1, source_target_pairs={{0,96},{1,33},{4,100},{5,37},{8,104},{9,41},{12,108},{13,45},{16,1... | collective-permute-start | bytes 3932168 | tf_op jit(solution)/shard_map/ppermute | solution.py:44
  75.4 32.1 %collective-permute-start.15 = (bf16[2,640,512]{2,1,0:T(8,128)(2,1)}, bf16[2,640,512]{2,1,0:T(8,128)(2,1)}, u32[]{:S(2)}, u32[]{:S(2)}) collective-permute-start(bf16[2,640,512]{2,1,0:T(8,128)(2,1)} %collective-permute-done.11.refs_11_.refs_7_), channel_id=1, source_target_pairs={{0,16},{1,17},{4,20},{5,21},{8,24},{9,25},{12,28},{13,29},{16,0},{... | collective-permute-start | bytes 3932168 | tf_op jit(solution)/shard_map/ppermute | solution.py:44
  77.0 39.0 %collective-permute-start.3 = (bf16[1280,640]{1,0:T(8,128)(2,1)}, bf16[1280,640]{1,0:T(8,128)(2,1)}, u32[]{:S(2)}, u32[]{:S(2)}) collective-permute-start(bf16[1280,640]{1,0:T(8,128)(2,1)} %collective-permute-done.refs_6_), channel_id=1, source_target_pairs={{0,4},{1,13},{4,8},{5,1},{8,12},{9,5},{12,0},{13,9},{16,20},{17,29... | collective-permute-start | bytes 4915208 | tf_op jit(solution)/shard_map/ppermute | solution.py:44
  81.8 38.0 %collective-permute-start.6 = (bf16[1280,640]{1,0:T(8,128)(2,1)}, bf16[1280,640]{1,0:T(8,128)(2,1)}, u32[]{:S(2)}, u32[]{:S(2)}) collective-permute-start(bf16[1280,640]{1,0:T(8,128)(2,1)} %collective-permute-done.5.refs_7_), channel_id=1, source_target_pairs={{0,12},{1,5},{4,0},{5,9},{8,4},{9,13},{12,8},{13,1},{16,28},{17,21... | collective-permute-start | bytes 4915208 | tf_op jit(solution)/shard_map/ppermute | solution.py:44
  125.9 6.3 %collective-permute-start.16 = (f32[1280,512]{1,0:T(8,128)}, f32[1280,512]{1,0:T(8,128)S(1)}, u32[]{:S(2)}, u32[]{:S(2)}) collective-permute-start(f32[1280,512]{1,0:T(8,128)} %shard_map.50), channel_id=1, source_target_pairs={{0,1},{1,0},{4,5},{5,4},{8,9},{9,8},{12,13},{13,12},{16,17},{17,16... | collective-permute-start | bytes 7864328 | tf_op jit(solution)/shard_map/ppermute | solution.py:44

commit v4 on v3

--- a/solution.py
+++ b/solution.py
@@ -263,7 +263,7 @@
     b0 = masked_half(first, shape_t, send(shape_t, SWAP), b, send(b, SWAP))
     z1 = send(b0, Z_AHEAD)
     z2 = send(b0, Z_BACK)
-    q = send(after(b0, x1), Y_NEAR)
+    q = send(after(b0, aq), Y_NEAR)
     x3 = send(x1, X_AHEAD)
     x5 = send(after(aq, x2), X_BACK)
     z3 = send(after(z1, z2), Z_AHEAD)
@@ -281,7 +281,7 @@
     near_plan = ((1, 0, False, 1), (1, 1, True, None), (0, 0, True, None))
     far_plan = ((0, 0, False, 1), (0, 1, True, None), (1, 0, True, None))
     sums = block_matmul(meta, int_shape, ready, near, (0, 1), near_plan, 2)
-    sums = block_matmul(meta, int_shape, ready, far, (0, 1), far_plan, 7, sums)
+    sums = block_matmul(meta, int_shape, ready, far, (0, 1), far_plan, 9, sums)
     late, late_plan = [groups[5], groups[7]], ((None, 0, True, None),)
     theirs = block_matmul(meta, int_shape, late, near + far, (1,), late_plan, 1, sums[1:])[0]
     got = send(theirs, SWAP)

time: 138 us -> 143 us (1.036); the launches traced: 135 us -> 142 us
  waiting for transfers between devices: 62.6 us -> 71.9 us
  starting transfers between devices: 30.5 us -> 28.1 us
    ppermute x17, waiting for transfers between devices: 62.6 us -> 71.9 us  [send(): return lax.ppermute(value, AXES, pairs)]
    ppermute x17, starting transfers between devices: 30.5 us -> 28.1 us  [send(): return lax.ppermute(value, AXES, pairs)]
  transfers between devices with their start and end apart: 17 -> 17, of which waited for: 8 -> 8; matrix products, arithmetic and copies ran while one was open for 1% -> 1% of each run, Pallas kernels for 22% -> 21%
where the time goes in v4:
time: 143 us; the launch traced here: 142 us
  waiting for transfers between devices  71.9 us (50%)
  Pallas kernels  36.3 us (25%)
  starting transfers between devices  28.1 us (20%)
  other arithmetic  3.83 us (3%)
  local copies, waits for them, and re-layouts  2.2 us (2%)
    ppermute x17, waiting for transfers between devices, send(): return lax.ppermute(value, AXES, pairs)  71.9 us
    pallas_call x4, Pallas kernels, block_matmul(): pl.pallas_call(functools.partial(block_kernel, spots, tuple(b_spots), tup...  33.1 us
    ppermute x17, starting transfers between devices, send(): return lax.ppermute(value, AXES, pairs)  28.1 us
    convert_element_type x1, other arithmetic, per_device(): return (ours + got).astype(jnp.bfloat16)  3.24 us
    pallas_call x1, Pallas kernels, masked_half(): pl.pallas_call(mask_kernel, out_shape=jax.ShapeDtypeStruct((2, *half), ow...  3.16 us
  transfers between devices with their start and end apart: 17, of which 8 were waited for; matrix products, arithmetic and copies ran while one was open for 1% of the time, Pallas kernels for 21%

profile of v4, /device:TPU:1, one launch (start us, length us, event | category | flops | bytes accessed | tf_op | source)
XLA Modules:
  0.0 142.4 jit_solution(16370177527215167966)
XLA Ops:
  0.0 1.4 collective-permute-start.8
  1.4 3.0 %collective-permute-start = (bf16[1280,640]{1,0:T(8,128)(2,1)}, bf16[1280,640]{1,0:T(8,128)(2,1)}, u32[]{:S(2)}, u32[]{:S(2)}) collective-permute-start(bf16[1280,640]{1,0:T(8,128)(2,1)} %refs_2_.3), channel_id=1, source_target_pairs={{0,2},{1,3},{4,6},{5,7},{8,10},{9,11},{12,14},{13,15},{16,18},{17,... | collective-permute-start | bytes 4915208 | tf_op jit(solution)/shard_map/ppermute | solution.py:44
  4.4 2.5 %collective-permute-start.1 = (bf16[1280,640]{1,0:T(8,128)(2,1)}, bf16[1280,640]{1,0:T(8,128)(2,1)}, u32[]{:S(2)}, u32[]{:S(2)}) collective-permute-start(bf16[1280,640]{1,0:T(8,128)(2,1)} %refs_2_.3), channel_id=1, source_target_pairs={{0,4},{1,13},{4,8},{5,1},{8,12},{9,5},{12,0},{13,9},{16,20},{17,29... | collective-permute-start | bytes 4915208 | tf_op jit(solution)/shard_map/ppermute | solution.py:44
  6.9 1.0 collective-permute-start.7
  7.9 0.6 pad_add_fusion.meta
  8.5 0.4 collective-permute-done.7.next_shape
  9.0 0.0 collective-permute-done.8.following
  9.0 0.5 copy-done.3
  9.5 1.1 copy-done.2
  10.6 3.2 %shard_map.46.refs_8_.refs_4_ = bf16[2,640,512]{2,1,0:T(8,128)(2,1)} custom-call(s32[2]{0:T(128)} %pad_add_fusion.meta, s32[2,40]{1,0:T(2,128)} %bitcast.21, s32[2,40]{1,0:T(2,128)} %copy-done.3, bf16[1280,512]{1,0:T(8,128)(2,1)} %own.1, bf16[1280,512]{1,0:T(8,128)(2,1)} %copy-done.2), custom_call_target="tpu_custom_call" | custom-call | bytes 2621440 | tf_op jit(solution)/shard_map/pallas_call | solution.py:78
  13.7 1.7 %collective-permute-start.10 = (bf16[2,640,512]{2,1,0:T(8,128)(2,1)}, bf16[2,640,512]{2,1,0:T(8,128)(2,1)S(1)}, u32[]{:S(2)}, u32[]{:S(2)}) collective-permute-start(bf16[2,640,512]{2,1,0:T(8,128)(2,1)} %shard_map.46.refs_8_.refs_4_), channel_id=1, source_target_pairs={{0,96},{1,33},{4,100},{5,37},{8,104},{9,41},{12,108},{13,45},{16,1... | collective-permute-start | bytes 3932168 | tf_op jit(solution)/shard_map/ppermute | solution.py:44
  15.4 2.2 %collective-permute-start.9 = (bf16[2,640,512]{2,1,0:T(8,128)(2,1)}, bf16[2,640,512]{2,1,0:T(8,128)(2,1)S(1)}, u32[]{:S(2)}, u32[]{:S(2)}) collective-permute-start(bf16[2,640,512]{2,1,0:T(8,128)(2,1)} %shard_map.46.refs_8_.refs_4_), channel_id=1, source_target_pairs={{0,32},{1,97},{4,36},{5,101},{8,40},{9,105},{12,44},{13,109},{16,4... | collective-permute-start | bytes 3932168 | tf_op jit(solution)/shard_map/ppermute | solution.py:44
  17.6 23.1 %collective-permute-done.refs_6_ = bf16[1280,640]{1,0:T(8,128)(2,1)} collective-permute-done((bf16[1280,640]{1,0:T(8,128)(2,1)}, bf16[1280,640]{1,0:T(8,128)(2,1)}, u32[]{:S(2)}, u32[]{:S(2)}) %collective-permute-start) | collective-permute-done | bytes 1638432 | tf_op jit(solution)/shard_map/ppermute | solution.py:44
  40.7 1.3 collective-permute-start.12
  42.1 1.2 collective-permute-done.10.refs_10_.refs_6_
  43.3 2.6 %collective-permute-done.9.refs_9_.refs_5_ = bf16[2,640,512]{2,1,0:T(8,128)(2,1)S(1)} collective-permute-done((bf16[2,640,512]{2,1,0:T(8,128)(2,1)}, bf16[2,640,512]{2,1,0:T(8,128)(2,1)S(1)}, u32[]{:S(2)}, u32[]{:S(2)}) %collective-permute-start.9) | collective-permute-done | bytes 1310752 | tf_op jit(solution)/shard_map/ppermute | solution.py:44
  45.9 3.3 %collective-permute-start.11 = (bf16[2,640,512]{2,1,0:T(8,128)(2,1)S(1)}, bf16[2,640,512]{2,1,0:T(8,128)(2,1)}, u32[]{:S(2)}, u32[]{:S(2)}) collective-permute-start(bf16[2,640,512]{2,1,0:T(8,128)(2,1)S(1)} %collective-permute-done.9.refs_9_.refs_5_), channel_id=1, source_target_pairs={{0,32},{1,97},{4,36},{5,101},{8,40},{9,105},{12,44},{13,109},{16,4... | collective-permute-start | bytes 3932168 | tf_op jit(solution)/shard_map/ppermute | solution.py:44
  49.2 2.2 %collective-permute-start.2 = (bf16[1280,640]{1,0:T(8,128)(2,1)}, bf16[1280,640]{1,0:T(8,128)(2,1)}, u32[]{:S(2)}, u32[]{:S(2)}) collective-permute-start(bf16[1280,640]{1,0:T(8,128)(2,1)} %collective-permute-done.1.refs_3_), channel_id=1, source_target_pairs={{0,4},{1,13},{4,8},{5,1},{8,12},{9,5},{12,0},{13,9},{16,20},{17,29... | collective-permute-start | bytes 4915208 | tf_op jit(solution)/shard_map/ppermute | solution.py:44
  51.4 19.3 %collective-permute-done.12.refs_8_ = bf16[2,640,512]{2,1,0:T(8,128)(2,1)} collective-permute-done((bf16[2,640,512]{2,1,0:T(8,128)(2,1)}, bf16[2,640,512]{2,1,0:T(8,128)(2,1)}, u32[]{:S(2)}, u32[]{:S(2)}) %collective-permute-start.12) | collective-permute-done | bytes 1310752 | tf_op jit(solution)/shard_map/ppermute | solution.py:44
  70.6 3.7 %collective-permute-start.13 = (bf16[2,640,512]{2,1,0:T(8,128)(2,1)}, bf16[2,640,512]{2,1,0:T(8,128)(2,1)}, u32[]{:S(2)}, u32[]{:S(2)}) collective-permute-start(bf16[2,640,512]{2,1,0:T(8,128)(2,1)} %collective-permute-done.12.refs_8_), channel_id=1, source_target_pairs={{0,32},{1,97},{4,36},{5,101},{8,40},{9,105},{12,44},{13,109},{16,4... | collective-permute-start | bytes 3932168 | tf_op jit(solution)/shard_map/ppermute | solution.py:44
  74.4 1.3 collective-permute-start.15
  75.7 11.3 %collective-permute-done.2.refs_5_ = bf16[1280,640]{1,0:T(8,128)(2,1)} collective-permute-done((bf16[1280,640]{1,0:T(8,128)(2,1)}, bf16[1280,640]{1,0:T(8,128)(2,1)}, u32[]{:S(2)}, u32[]{:S(2)}) %collective-permute-start.2) | collective-permute-done | bytes 1638432 | tf_op jit(solution)/shard_map/ppermute | solution.py:44
  86.9 3.4 %collective-permute-start.3 = (bf16[1280,640]{1,0:T(8,128)(2,1)}, bf16[1280,640]{1,0:T(8,128)(2,1)}, u32[]{:S(2)}, u32[]{:S(2)}) collective-permute-start(bf16[1280,640]{1,0:T(8,128)(2,1)} %collective-permute-done.refs_6_), channel_id=1, source_target_pairs={{0,4},{1,13},{4,8},{5,1},{8,12},{9,5},{12,0},{13,9},{16,20},{17,29... | collective-permute-start | bytes 4915208 | tf_op jit(solution)/shard_map/ppermute | solution.py:44
  90.4 0.6 stack.86.refs_0_
  91.0 12.2 %shard_map.47 = (f32[1280,512]{1,0:T(8,128)}, f32[1280,512]{1,0:T(8,128)}) custom-call(s32[18]{0:T(128)} %stack.86.refs_0_, s32[5,40]{1,0:T(8,128)} %refs_1_.7, bf16[1280,640]{1,0:T(8,128)(2,1)} %refs_2_.3, bf16[1280,640]{1,0:T(8,128)(2,1)} %collective-permute-done.1.refs_3_, bf16[1280,640]{1,0:T(8,128)(2,1)} %collective-permute-done.4.refs_4_, ...), custom_call_target="tpu_custom_call" | custom-call | flops 1677721600 | bytes 1638400 | tf_op jit(solution)/shard_map/pallas_call | solution.py:221
  103.3 2.6 %collective-permute-done.14.refs_10_ = bf16[2,640,512]{2,1,0:T(8,128)(2,1)} collective-permute-done((bf16[2,640,512]{2,1,0:T(8,128)(2,1)}, bf16[2,640,512]{2,1,0:T(8,128)(2,1)}, u32[]{:S(2)}, u32[]{:S(2)}) %collective-permute-start.14) | collective-permute-done | bytes 1310752 | tf_op jit(solution)/shard_map/ppermute | solution.py:44
  105.9 8.5 %shard_map.48 = (f32[1280,512]{1,0:T(8,128)}, f32[1280,512]{1,0:T(8,128)}) custom-call(s32[18]{0:T(128)} %stack.86.refs_0_, s32[5,40]{1,0:T(8,128)} %refs_1_.7, bf16[1280,640]{1,0:T(8,128)(2,1)} %refs_2_.3, bf16[1280,640]{1,0:T(8,128)(2,1)} %collective-permute-done.1.refs_3_, bf16[1280,640]{1,0:T(8,128)(2,1)} %collective-permute-done.4.refs_4_, ...), custom_call_target="tpu_custom_call" | custom-call | flops 7549747200 | bytes 1638400 | tf_op jit(solution)/shard_map/pallas_call | solution.py:221
  114.4 11.4 %collective-permute-done.3.refs_2_ = bf16[1280,640]{1,0:T(8,128)(2,1)} collective-permute-done((bf16[1280,640]{1,0:T(8,128)(2,1)}, bf16[1280,640]{1,0:T(8,128)(2,1)}, u32[]{:S(2)}, u32[]{:S(2)}) %collective-permute-start.3) | collective-permute-done | bytes 1638432 | tf_op jit(solution)/shard_map/ppermute | solution.py:44
  125.8 6.2 %shard_map.50 = f32[1280,512]{1,0:T(8,128)} custom-call(s32[18]{0:T(128)} %stack.86.refs_0_, s32[5,40]{1,0:T(8,128)} %refs_1_.7, bf16[1280,640]{1,0:T(8,128)(2,1)} %collective-permute-done.3.refs_2_, bf16[1280,640]{1,0:T(8,128)(2,1)} %collective-permute-done.6.refs_3_, bf16[2,640,512]{2,1,0:T(8,128)(2,1)} %shard_map.46.refs_8_.refs_4_, ...), custom_call_target="tpu_custom_call" | custom-call | flops 838860800 | bytes 1638400 | tf_op jit(solution)/shard_map/pallas_call | solution.py:221
  132.0 0.9 collective-permute-start.16
  133.0 6.2 %shard_map.49 = f32[1280,512]{1,0:T(8,128)} custom-call(s32[18]{0:T(128)} %stack.86.refs_0_, s32[5,40]{1,0:T(8,128)} %refs_1_.7, bf16[1280,640]{1,0:T(8,128)(2,1)} %collective-permute-done.3.refs_2_, bf16[1280,640]{1,0:T(8,128)(2,1)} %collective-permute-done.6.refs_3_, bf16[2,640,512]{2,1,0:T(8,128)(2,1)} %shard_map.46.refs_8_.refs_4_, ...), custom_call_target="tpu_custom_call" | custom-call | flops 838860800 | bytes 1638400 | tf_op jit(solution)/shard_map/pallas_call | solution.py:221
  139.2 3.2 %add_convert_fusion = bf16[1280,512]{1,0:T(8,128)(2,1)} fusion(f32[1280,512]{1,0:T(8,128)} %shard_map.49, f32[1280,512]{1,0:T(8,128)S(1)} %collective-permute-done.16), kind=kLoop, calls=%fused_computation | loop fusion | flops 1310720 | bytes 6553600 | tf_op jit(solution)/shard_map/convert_element_type | solution.py:289
  (18 shorter events, 0.0 us)
Async XLA Ops:
  0.0 9.0 %collective-permute-start.8 = (bf16[1280,512]{1,0:T(8,128)(2,1)}, bf16[1280,512]{1,0:T(8,128)(2,1)S(1)}, u32[]{:S(2)}, u32[]{:S(2)}) collective-permute-start(bf16[1280,512]{1,0:T(8,128)(2,1)} %own.1), channel_id=1, source_target_pairs={{0,1},{1,0},{4,5},{5,4},{8,9},{9,8},{12,13},{13,12},{16,17},{17,16... | collective-permute-start | bytes 3932168 | tf_op jit(solution)/shard_map/ppermute | solution.py:44
  1.4 39.3 %collective-permute-start = (bf16[1280,640]{1,0:T(8,128)(2,1)}, bf16[1280,640]{1,0:T(8,128)(2,1)}, u32[]{:S(2)}, u32[]{:S(2)}) collective-permute-start(bf16[1280,640]{1,0:T(8,128)(2,1)} %refs_2_.3), channel_id=1, source_target_pairs={{0,2},{1,3},{4,6},{5,7},{8,10},{9,11},{12,14},{13,15},{16,18},{17,... | collective-permute-start | bytes 4915208 | tf_op jit(solution)/shard_map/ppermute | solution.py:44
  4.4 44.8 %collective-permute-start.1 = (bf16[1280,640]{1,0:T(8,128)(2,1)}, bf16[1280,640]{1,0:T(8,128)(2,1)}, u32[]{:S(2)}, u32[]{:S(2)}) collective-permute-start(bf16[1280,640]{1,0:T(8,128)(2,1)} %refs_2_.3), channel_id=1, source_target_pairs={{0,4},{1,13},{4,8},{5,1},{8,12},{9,5},{12,0},{13,9},{16,20},{17,29... | collective-permute-start | bytes 4915208 | tf_op jit(solution)/shard_map/ppermute | solution.py:44
  6.9 44.5 %collective-permute-start.4 = (bf16[1280,640]{1,0:T(8,128)(2,1)}, bf16[1280,640]{1,0:T(8,128)(2,1)}, u32[]{:S(2)}, u32[]{:S(2)}) collective-permute-start(bf16[1280,640]{1,0:T(8,128)(2,1)} %refs_2_.3), channel_id=1, source_target_pairs={{0,12},{1,5},{4,0},{5,9},{8,4},{9,13},{12,8},{13,1},{16,28},{17,21... | collective-permute-start | bytes 4915208 | tf_op jit(solution)/shard_map/ppermute | solution.py:44
  6.9 2.1 %collective-permute-start.7 = (s32[2,40]{1,0:T(2,128)}, s32[2,40]{1,0:T(2,128)S(1)}, u32[]{:S(2)}, u32[]{:S(2)}) collective-permute-start(s32[2,40]{1,0:T(2,128)} %bitcast.20), channel_id=1, source_target_pairs={{0,1},{1,0},{4,5},{5,4},{8,9},{9,8},{12,13},{13,12},{16,17},{17,16... | collective-permute-start | bytes 968 | tf_op jit(solution)/shard_map/ppermute | solution.py:44
  9.0 0.5 copy-start.3
  9.5 1.1 copy-start.2
  13.7 29.6 %collective-permute-start.10 = (bf16[2,640,512]{2,1,0:T(8,128)(2,1)}, bf16[2,640,512]{2,1,0:T(8,128)(2,1)S(1)}, u32[]{:S(2)}, u32[]{:S(2)}) collective-permute-start(bf16[2,640,512]{2,1,0:T(8,128)(2,1)} %shard_map.46.refs_8_.refs_4_), channel_id=1, source_target_pairs={{0,96},{1,33},{4,100},{5,37},{8,104},{9,41},{12,108},{13,45},{16,1... | collective-permute-start | bytes 3932168 | tf_op jit(solution)/shard_map/ppermute | solution.py:44
  15.4 30.5 %collective-permute-start.9 = (bf16[2,640,512]{2,1,0:T(8,128)(2,1)}, bf16[2,640,512]{2,1,0:T(8,128)(2,1)S(1)}, u32[]{:S(2)}, u32[]{:S(2)}) collective-permute-start(bf16[2,640,512]{2,1,0:T(8,128)(2,1)} %shard_map.46.refs_8_.refs_4_), channel_id=1, source_target_pairs={{0,32},{1,97},{4,36},{5,101},{8,40},{9,105},{12,44},{13,109},{16,4... | collective-permute-start | bytes 3932168 | tf_op jit(solution)/shard_map/ppermute | solution.py:44
  40.7 29.9 %collective-permute-start.12 = (bf16[2,640,512]{2,1,0:T(8,128)(2,1)}, bf16[2,640,512]{2,1,0:T(8,128)(2,1)}, u32[]{:S(2)}, u32[]{:S(2)}) collective-permute-start(bf16[2,640,512]{2,1,0:T(8,128)(2,1)} %shard_map.46.refs_8_.refs_4_), channel_id=1, source_target_pairs={{0,16},{1,17},{4,20},{5,21},{8,24},{9,25},{12,28},{13,29},{16,0},{... | collective-permute-start | bytes 3932168 | tf_op jit(solution)/shard_map/ppermute | solution.py:44
  43.3 47.7 %copy-start = (bf16[2,640,512]{2,1,0:T(8,128)(2,1)}, bf16[2,640,512]{2,1,0:T(8,128)(2,1)S(1)}, u32[]{:S(2)}) copy-start(bf16[2,640,512]{2,1,0:T(8,128)(2,1)S(1)} %collective-permute-done.10.refs_10_.refs_6_) | copy-start | bytes 3932164
  45.9 45.1 %copy-start.1 = (bf16[2,640,512]{2,1,0:T(8,128)(2,1)}, bf16[2,640,512]{2,1,0:T(8,128)(2,1)S(1)}, u32[]{:S(2)}) copy-start(bf16[2,640,512]{2,1,0:T(8,128)(2,1)S(1)} %collective-permute-done.9.refs_9_.refs_5_) | copy-start | bytes 3932164
  45.9 24.7 %collective-permute-start.11 = (bf16[2,640,512]{2,1,0:T(8,128)(2,1)S(1)}, bf16[2,640,512]{2,1,0:T(8,128)(2,1)}, u32[]{:S(2)}, u32[]{:S(2)}) collective-permute-start(bf16[2,640,512]{2,1,0:T(8,128)(2,1)S(1)} %collective-permute-done.9.refs_9_.refs_5_), channel_id=1, source_target_pairs={{0,32},{1,97},{4,36},{5,101},{8,40},{9,105},{12,44},{13,109},{16,4... | collective-permute-start | bytes 3932168 | tf_op jit(solution)/shard_map/ppermute | solution.py:44
  49.2 37.7 %collective-permute-start.2 = (bf16[1280,640]{1,0:T(8,128)(2,1)}, bf16[1280,640]{1,0:T(8,128)(2,1)}, u32[]{:S(2)}, u32[]{:S(2)}) collective-permute-start(bf16[1280,640]{1,0:T(8,128)(2,1)} %collective-permute-done.1.refs_3_), channel_id=1, source_target_pairs={{0,4},{1,13},{4,8},{5,1},{8,12},{9,5},{12,0},{13,9},{16,20},{17,29... | collective-permute-start | bytes 4915208 | tf_op jit(solution)/shard_map/ppermute | solution.py:44
  51.4 39.0 %collective-permute-start.5 = (bf16[1280,640]{1,0:T(8,128)(2,1)}, bf16[1280,640]{1,0:T(8,128)(2,1)}, u32[]{:S(2)}, u32[]{:S(2)}) collective-permute-start(bf16[1280,640]{1,0:T(8,128)(2,1)} %collective-permute-done.refs_6_), channel_id=1, source_target_pairs={{0,12},{1,5},{4,0},{5,9},{8,4},{9,13},{12,8},{13,1},{16,28},{17,21... | collective-permute-start | bytes 4915208 | tf_op jit(solution)/shard_map/ppermute | solution.py:44
  70.6 32.6 %collective-permute-start.13 = (bf16[2,640,512]{2,1,0:T(8,128)(2,1)}, bf16[2,640,512]{2,1,0:T(8,128)(2,1)}, u32[]{:S(2)}, u32[]{:S(2)}) collective-permute-start(bf16[2,640,512]{2,1,0:T(8,128)(2,1)} %collective-permute-done.12.refs_8_), channel_id=1, source_target_pairs={{0,32},{1,97},{4,36},{5,101},{8,40},{9,105},{12,44},{13,109},{16,4... | collective-permute-start | bytes 3932168 | tf_op jit(solution)/shard_map/ppermute | solution.py:44
  74.4 31.5 %collective-permute-start.14 = (bf16[2,640,512]{2,1,0:T(8,128)(2,1)}, bf16[2,640,512]{2,1,0:T(8,128)(2,1)}, u32[]{:S(2)}, u32[]{:S(2)}) collective-permute-start(bf16[2,640,512]{2,1,0:T(8,128)(2,1)} %collective-permute-done.12.refs_8_), channel_id=1, source_target_pairs={{0,96},{1,33},{4,100},{5,37},{8,104},{9,41},{12,108},{13,45},{16,1... | collective-permute-start | bytes 3932168 | tf_op jit(solution)/shard_map/ppermute | solution.py:44
  74.4 31.5 %collective-permute-start.15 = (bf16[2,640,512]{2,1,0:T(8,128)(2,1)}, bf16[2,640,512]{2,1,0:T(8,128)(2,1)}, u32[]{:S(2)}, u32[]{:S(2)}) collective-permute-start(bf16[2,640,512]{2,1,0:T(8,128)(2,1)} %collective-permute-done.11.refs_11_.refs_7_), channel_id=1, source_target_pairs={{0,16},{1,17},{4,20},{5,21},{8,24},{9,25},{12,28},{13,29},{16,0},{... | collective-permute-start | bytes 3932168 | tf_op jit(solution)/shard_map/ppermute | solution.py:44
  86.9 38.9 %collective-permute-start.3 = (bf16[1280,640]{1,0:T(8,128)(2,1)}, bf16[1280,640]{1,0:T(8,128)(2,1)}, u32[]{:S(2)}, u32[]{:S(2)}) collective-permute-start(bf16[1280,640]{1,0:T(8,128)(2,1)} %collective-permute-done.refs_6_), channel_id=1, source_target_pairs={{0,4},{1,13},{4,8},{5,1},{8,12},{9,5},{12,0},{13,9},{16,20},{17,29... | collective-permute-start | bytes 4915208 | tf_op jit(solution)/shard_map/ppermute | solution.py:44
  90.4 35.5 %collective-permute-start.6 = (bf16[1280,640]{1,0:T(8,128)(2,1)}, bf16[1280,640]{1,0:T(8,128)(2,1)}, u32[]{:S(2)}, u32[]{:S(2)}) collective-permute-start(bf16[1280,640]{1,0:T(8,128)(2,1)} %collective-permute-done.5.refs_7_), channel_id=1, source_target_pairs={{0,12},{1,5},{4,0},{5,9},{8,4},{9,13},{12,8},{13,1},{16,28},{17,21... | collective-permute-start | bytes 4915208 | tf_op jit(solution)/shard_map/ppermute | solution.py:44
  132.0 7.1 %collective-permute-start.16 = (f32[1280,512]{1,0:T(8,128)}, f32[1280,512]{1,0:T(8,128)S(1)}, u32[]{:S(2)}, u32[]{:S(2)}) collective-permute-start(f32[1280,512]{1,0:T(8,128)} %shard_map.50), channel_id=1, source_target_pairs={{0,1},{1,0},{4,5},{5,4},{8,9},{9,8},{12,13},{13,12},{16,17},{17,16... | collective-permute-start | bytes 7864328 | tf_op jit(solution)/shard_map/ppermute | solution.py:44
